TPU v7x, 128 devices: a whole 4x4x4 slice. The times are simulated.
128 devices in a mesh: blk: 32 (over x, y, z_lo), segment: 4 (over z_hi, core).
Axes of the slice: x: 4, y: 4, z: 4 (z_hi: 2, z_lo: 2; z = z_hi * 2 + z_lo), core: 2. Of those that a mesh axis runs over, the one named last changes fastest.
Arguments:
- latent_queries: bfloat16 [2, 128, 2048], P(None, 'blk'), may hold values from -400 to 400
- latent_embed: bfloat16 [2, 128, 2048], P(None, 'blk'), may hold values from -6 to 6
- history_keys: bfloat16 [2, 32768, 2048], P(None, ('blk', 'segment')), may hold values from -6 to 6
- history_values: bfloat16 [2, 32768, 2048], P(None, ('blk', 'segment')), may hold values from -7 to 7
- latent_pos: int32 [2, 128], replicated, may hold values from 1 to 32768, as said below
- norm_gain: float32 [4, 2048], P('segment'), may hold values from 0.25 to 1.75
- w_qkv: bfloat16 [4, 2048, 3, 2048], P('segment', None, None, 'blk'), may hold values from -0.125 to 0.125
- w_out: bfloat16 [4, 2048, 2048], P('segment', 'blk'), may hold values from -0.125 to 0.125
Outputs:
- latents_out: float32 [2, 128, 2048], P(None, 'blk', 'segment')
Inputs may be any that keep to these rules, and one draw needn't show every extreme that they name: `latent_pos`: Non-decreasing along the latents of a micro-batch; latent i sees at least (i + 1) * 256 positions and the last latent sees all 32768.
All inputs are finite; a program needn't handle non-finite values.
Results may differ from a plain program's by a relative error of at most 0.0085.
Values may be sent and summed in bfloat16 or wider, within the bound.
A program may use at most 64 MiB of HBM per device.

v0:
```python
import jax
import jax.numpy as jnp
from jax import lax
from jax.sharding import PartitionSpec as P

HEADS = 16


epsilon = 1e-06
masked = -1e30


def from_partner(array, axis, distance):
    return lax.ppermute(array, axis, [(i, i ^ 1 << distance) for i in range(lax.axis_size(axis))])


def shifted(value, axis, steps):
    count = lax.axis_size(axis)
    first, last = (max(0, -steps), min(count, count - steps))
    return lax.ppermute(value, axis, [(source, source + steps) for source in range(first, last)])


def normalize(latent_state, gain_row):
    factor = lax.rsqrt(jnp.mean(latent_state * latent_state, axis=1, keepdims=True) + epsilon)
    return (latent_state * factor * gain_row).astype(jnp.bfloat16)


def attend_columns(mixed_qkv, head_size):
    lat_count = mixed_qkv.shape[0]
    columns = mixed_qkv.shape[1] // 3
    head_span = min(columns, head_size)
    head_groups = columns // head_span
    query_part = mixed_qkv[:, :columns].reshape(lat_count, head_groups, head_span)
    key_part = mixed_qkv[:, columns : 2 * columns].reshape(lat_count, head_groups, head_span)
    value_part = mixed_qkv[:, 2 * columns :].reshape(lat_count, head_groups, head_span)
    scores = jnp.einsum("ipd,jpd->pij", query_part, key_part, preferred_element_type=jnp.float32)
    scores = scores + from_partner(scores, "blk", 0)
    scores = scores * head_size ** (-0.5)
    row_ids = lax.broadcasted_iota(jnp.int32, (lat_count, lat_count), 0)
    col_ids = lax.broadcasted_iota(jnp.int32, (lat_count, lat_count), 1)
    scores = jnp.where((col_ids <= row_ids)[None], scores, masked)
    row_top = jnp.max(scores, axis=2, keepdims=True)
    weights = jnp.exp(scores - row_top)
    soft_weights = (weights / jnp.sum(weights, axis=2, keepdims=True)).astype(jnp.bfloat16)
    attended = jnp.einsum(
        "pij,jpd->ipd", soft_weights, value_part, preferred_element_type=jnp.float32
    )
    return attended.reshape(lat_count, columns).astype(jnp.bfloat16)


def layer_full(latent_state, gain_row, projection, output_rows, head_size):
    normed = normalize(latent_state, gain_row)
    mixed_qkv = jnp.dot(normed, projection, preferred_element_type=jnp.float32).astype(jnp.bfloat16)
    attended = attend_columns(mixed_qkv, head_size)
    update = jnp.dot(attended, output_rows, preferred_element_type=jnp.float32)
    return latent_state + lax.psum(update, "blk")


def on_device(
    latent_queries, latent_embed, history_keys, history_values, latent_pos, norm_gain, w_qkv, w_out
):
    segment_count = lax.axis_size("segment")
    blk_id = lax.axis_index("blk")
    segment_id = lax.axis_index("segment")
    micro_count = history_keys.shape[0]
    hist_rows = history_keys.shape[1]
    width = history_keys.shape[2]
    head_size = width // HEADS
    gathered = lax.all_gather(latent_queries, "blk", axis=1, tiled=True)
    lat_count = gathered.shape[1]
    first_key = (blk_id * segment_count + segment_id) * hist_rows
    key_ids = first_key + jnp.arange(hist_rows, dtype=jnp.int32)
    visible = (key_ids[None, None, :] < latent_pos[:, :, None])[:, None]
    query_heads = gathered.reshape(micro_count, lat_count, HEADS, head_size)
    key_heads = history_keys.reshape(micro_count, hist_rows, HEADS, head_size)
    value_heads = history_values.reshape(micro_count, hist_rows, HEADS, head_size)
    scores = jnp.einsum(
        "mqhd,mkhd->mhqk", query_heads, key_heads, preferred_element_type=jnp.float32
    ) * head_size ** (-0.5)
    scores = jnp.where(visible, scores, masked)
    highest = lax.pmax(jnp.max(scores, axis=3), ("blk", "segment"))
    weights = jnp.where(visible, jnp.exp(scores - highest[..., None]), 0.0)
    totals = jnp.transpose(jnp.sum(weights, axis=3), (0, 2, 1))
    partial_value = jnp.einsum(
        "mhqk,mkhd->mqhd",
        weights.astype(jnp.bfloat16),
        value_heads,
        preferred_element_type=jnp.float32,
    )
    partial_value = partial_value.reshape(micro_count, lat_count, width)
    summed, counted = (
        lax.psum_scatter(partial_value, "blk", scatter_dimension=1, tiled=True),
        lax.psum_scatter(totals, "blk", scatter_dimension=1, tiled=True),
    )
    summed, counted = lax.psum((summed, counted), "segment")
    rows_here = summed.shape[1]
    attended = (
        summed.reshape(micro_count, rows_here, HEADS, head_size) / counted[..., None]
    ).reshape(micro_count, rows_here, width)
    start_state = latent_embed.astype(jnp.float32) + attended
    gain_row = norm_gain[0]
    projection = w_qkv[0].reshape(width, -1)
    output_rows = w_out[0]
    tower_in = lax.all_gather(start_state, "blk", axis=1, tiled=True)
    rounds = micro_count + segment_count - 1
    last_segment = segment_count - 1
    incoming = jnp.zeros_like(tower_in[0])
    finished = []
    for round_index in range(rounds):
        if round_index < micro_count:
            incoming = jnp.where(segment_id == 0, tower_in[round_index], incoming)
        latent_state = layer_full(incoming, gain_row, projection, output_rows, head_size)
        if round_index >= last_segment:
            finished.append(jnp.where(segment_id == last_segment, latent_state, 0.0))
        if round_index + 1 < rounds:
            incoming = shifted(latent_state, "segment", 1)
    results = jnp.stack(finished)
    own_rows = latent_embed.shape[1]
    results = lax.dynamic_slice_in_dim(results, blk_id * own_rows, own_rows, 1)
    return lax.psum_scatter(results, "segment", scatter_dimension=2, tiled=True)


def solution(mesh):
    return jax.shard_map(
        on_device,
        mesh=mesh,
        in_specs=(
            P(None, "blk", None),
            P(None, "blk", None),
            P(None, ("blk", "segment"), None),
            P(None, ("blk", "segment"), None),
            P(),
            P("segment", None),
            P("segment", None, None, "blk"),
            P("segment", "blk", None),
        ),
        out_specs=P(None, "blk", "segment"),
        check_vma=False,
    )
```

profile of v0, /device:TPU:1, one launch (start us, length us, event | category | flops | bytes accessed | tf_op | source)
XLA Modules:
  0.0 2481.4 jit_solution(8695598158295302768)
XLA Ops:
  6.5 1.6 copy.17
  8.2 4.0 copy.28
  12.3 127.7 %all-gather.3.cloned.1.call-done = bf16[2,128,2048]{2,0,1:T(2,128)(2,1)} async-done(((bf16[2,4,2048]{2,0,1:T(2,128)(2,1)}), bf16[2,128,2048]{2,0,1:T(2,128)(2,1)}) %all-gather.3.cloned.1.call-update) | async-done | bytes 1048592 | tf_op jit(solution)/shard_map/all_gather | solution.py:69
  139.9 3.7 copy.18
  143.6 4.4 fusion
  148.0 87.3 %pmax.7 = f32[2,16,128]{2,1,0:T(8,128)S(1)} all-reduce(f32[2,16,128]{2,1,0:T(8,128)S(1)} %get-tuple-element.11), channel_id=1, replica_groups=mesh['blk'=32,'segment'=4] {'blk','segment'}, use_global_device_ids=true, to_apply=%region_1.2 | all-reduce | flops 4096 | bytes 32768 | tf_op jit(solution)/shard_map/pmax | solution.py:81
  235.3 5.4 fusion.3
  240.7 2.9 copy.22
  243.7 0.6 dynamic-slice
  245.0 3.1 fusion.1
  248.2 131.5 %all-reduce.1 = f32[2,128,16]{2,1,0:T(8,128)S(1)} all-reduce(f32[2,128,16]{2,1,0:T(8,128)S(1)} %copy.23), channel_id=3, replica_groups=mesh['blk'=32,'segment'=4] {'blk'}, use_global_device_ids=true, to_apply=%region_5.6.clone | all-reduce | flops 4096 | bytes 32768
  379.8 153.2 %all-reduce.22.cloned.1.call-done = f32[2,128,2048]{2,1,0:T(8,128)} async-done(((f32[2,128,2048]{2,1,0:T(8,128)}), f32[2,128,2048]{2,1,0:T(8,128)}) %all-reduce.22.cloned.1.call-update) | async-done | bytes 2097168
  533.0 1.5 constant_dynamic-slice_fusion.1
  534.6 29.4 %psum.50 = f32[2,4,16]{2,1,0:T(4,128)S(1)} all-reduce(f32[2,4,16]{2,1,0:T(4,128)S(1)} %constant_dynamic-slice_fusion), channel_id=1, replica_groups=mesh['blk'=32,'segment'=4] {'segment'}, use_global_device_ids=true, to_apply=%region_6.7 | all-reduce | flops 128 | bytes 1024 | tf_op jit(solution)/shard_map/psum | solution.py:95
  564.2 34.6 %all-reduce.10.cloned.1.call-done = f32[2,4,2048]{2,1,0:T(4,128)} async-done(((f32[2,4,2048]{2,1,0:T(4,128)}), f32[2,4,2048]{2,1,0:T(4,128)}) %all-reduce.10.cloned.1.call-update) | async-done | bytes 65552 | tf_op jit(solution)/shard_map/psum | solution.py:95
  598.8 0.9 divide_add_fusion
  599.6 0.7 copy.24
  600.4 128.9 %all-gather.5.cloned.1.call-done = f32[2,128,2048]{2,0,1:T(2,128)} async-done(((f32[2,4,2048]{2,0,1:T(2,128)}), f32[2,128,2048]{2,0,1:T(2,128)}) %all-gather.5.cloned.1.call-update) | async-done | bytes 2097168 | tf_op jit(solution)/shard_map/all_gather | solution.py:104
  729.2 5.4 fusion.100
  735.0 0.5 copy-done.6
  735.6 0.6 convolution_convert_fusion.4
  736.4 1.4 collective-permute-start
  737.8 2.3 collective-permute-done
  740.2 1.5 fusion.14
  741.7 311.0 %all-reduce.12.cloned.1.call-done = f32[128,2048]{1,0:T(8,128)} async-done(((f32[128,2048]{1,0:T(8,128)}), f32[128,2048]{1,0:T(8,128)}) %all-reduce.12.cloned.1.call-update) | async-done | bytes 1048592 | tf_op jit(solution)/shard_map/psum | solution.py:56
  1052.8 2.0 bitcast_add_fusion
  1054.8 28.3 %collective-permute-start.1 = (f32[128,2048]{1,0:T(8,128)S(1)}, f32[128,2048]{1,0:T(8,128)S(1)}, u32[]{:S(2)}, u32[]{:S(2)}) collective-permute-start(f32[128,2048]{1,0:T(8,128)S(1)} %bitcast_add_fusion), channel_id=1, source_target_pairs={{0,1},{1,2},{2,3},{4,5},{5,6},{6,7},{8,9},{9,10},{10,11},{12,13},{... | collective-permute-start | bytes 3145736 | tf_op jit(solution)/shard_map/ppermute | solution.py:20
  1083.1 12.2 collective-permute-done.1
  1095.4 1.9 multiply_reduce_fusion.3
  1097.3 1.0 copy-done.4
  1098.2 0.5 convolution_convert_fusion.3
  1099.4 2.8 collective-permute-done.2
  1102.2 1.5 fusion.16
  1103.7 289.7 %all-reduce.14.cloned.1.call-done = f32[128,2048]{1,0:T(8,128)} async-done(((f32[128,2048]{1,0:T(8,128)}), f32[128,2048]{1,0:T(8,128)}) %all-reduce.14.cloned.1.call-update) | async-done | bytes 1048592 | tf_op jit(solution)/shard_map/psum | solution.py:56
  1393.4 1.7 add.118
  1395.1 28.1 %collective-permute-start.3 = (f32[128,2048]{1,0:T(8,128)S(1)}, f32[128,2048]{1,0:T(8,128)S(1)}, u32[]{:S(2)}, u32[]{:S(2)}) collective-permute-start(f32[128,2048]{1,0:T(8,128)S(1)} %add.118), channel_id=1, source_target_pairs={{0,1},{1,2},{2,3},{4,5},{5,6},{6,7},{8,9},{9,10},{10,11},{12,13},{... | collective-permute-start | bytes 3145736 | tf_op jit(solution)/shard_map/ppermute | solution.py:20
  1423.2 12.4 collective-permute-done.3
  1435.8 0.8 copy-done.3
  1436.6 0.5 convolution_convert_fusion.2
  1437.7 2.8 collective-permute-done.4
  1440.6 1.5 fusion.18
  1442.1 289.7 %all-reduce.16.cloned.1.call-done = f32[128,2048]{1,0:T(8,128)} async-done(((f32[128,2048]{1,0:T(8,128)}), f32[128,2048]{1,0:T(8,128)}) %all-reduce.16.cloned.1.call-update) | async-done | bytes 1048592 | tf_op jit(solution)/shard_map/psum | solution.py:56
  1731.8 1.7 add.121
  1733.5 28.1 %collective-permute-start.5 = (f32[128,2048]{1,0:T(8,128)S(1)}, f32[128,2048]{1,0:T(8,128)S(1)}, u32[]{:S(2)}, u32[]{:S(2)}) collective-permute-start(f32[128,2048]{1,0:T(8,128)S(1)} %add.121), channel_id=1, source_target_pairs={{0,1},{1,2},{2,3},{4,5},{5,6},{6,7},{8,9},{9,10},{10,11},{12,13},{... | collective-permute-start | bytes 3145736 | tf_op jit(solution)/shard_map/ppermute | solution.py:20
  1761.6 12.4 collective-permute-done.5
  1774.2 0.9 copy-done.2
  1775.1 0.5 convolution_convert_fusion.1
  1776.2 2.8 collective-permute-done.6
  1779.0 1.5 fusion.20
  1780.6 289.6 %all-reduce.18.cloned.1.call-done = f32[128,2048]{1,0:T(8,128)} async-done(((f32[128,2048]{1,0:T(8,128)}), f32[128,2048]{1,0:T(8,128)}) %all-reduce.18.cloned.1.call-update) | async-done | bytes 1048592 | tf_op jit(solution)/shard_map/psum | solution.py:56
  2070.2 2.7 select_bitcast_fusion.1
  2072.9 28.1 %collective-permute-start.7 = (f32[128,2048]{1,0:T(8,128)S(1)}, f32[128,2048]{1,0:T(8,128)S(1)}, u32[]{:S(2)}, u32[]{:S(2)}) collective-permute-start(f32[128,2048]{1,0:T(8,128)S(1)} %get-tuple-element.6), channel_id=1, source_target_pairs={{0,1},{1,2},{2,3},{4,5},{5,6},{6,7},{8,9},{9,10},{10,11},{12,13},{... | collective-permute-start | bytes 3145736 | tf_op jit(solution)/shard_map/ppermute | solution.py:20
  2101.0 12.4 collective-permute-done.7
  2113.6 0.5 convolution_convert_fusion
  2115.1 2.8 collective-permute-done.8
  2117.9 1.5 fusion.22
  2119.5 289.7 %all-reduce.20.cloned.1.call-done = f32[128,2048]{1,0:T(8,128)} async-done(((f32[128,2048]{1,0:T(8,128)}), f32[128,2048]{1,0:T(8,128)}) %all-reduce.20.cloned.1.call-update) | async-done | bytes 1048592 | tf_op jit(solution)/shard_map/psum | solution.py:56
  2409.2 1.7 select_bitcast_fusion
  2410.8 0.9 fusion.44
  2411.7 2.3 copy.33
  2414.0 3.3 reshape.239
  2417.4 55.1 %reduce-scatter.6.cloned.1.call-done = f32[512,8]{1,0:T(8,128)} async-done(((f32[2048,8]{1,0:T(8,128)}), f32[512,8]{1,0:T(8,128)}) %reduce-scatter.6.cloned.1.call-update) | async-done | bytes 16400
  2472.5 1.3 reshape.240
  2473.8 0.8 copy.34
  (74 shorter events, 5.4 us)
Async XLA Ops:
  6.5 137.1 %copy-start = (bf16[2,256,2048]{2,1,0:T(8,128)(2,1)S(1)}, bf16[2,256,2048]{2,1,0:T(8,128)(2,1)}, u32[]{:S(2)}) copy-start(bf16[2,256,2048]{2,1,0:T(8,128)(2,1)} %param.10) | copy-start | bytes 6291460
  6.5 5.6 copy-start.10
  6.5 133.4 %all-gather.3.cloned.1.call-start = ((), (), s32[]{:S(2)}) async-start(), calls=%async_computation.1 | async-start | bytes 1081344 | tf_op jit(solution)/shard_map/all_gather | solution.py:69
  8.1 524.9 %all-reduce.22.cloned.1.call-start = ((), (), s32[]{:S(2)}) async-start(), calls=%async_computation.10 | async-start | bytes 4194304
  240.7 3.0 copy-start.11
  243.6 355.1 %copy-start.9 = (bf16[2,4,2048]{2,1,0:T(4,128)(2,1)S(1)}, bf16[2,4,2048]{2,1,0:T(4,128)(2,1)}, u32[]{:S(2)}) copy-start(bf16[2,4,2048]{2,1,0:T(4,128)(2,1)} %param.9) | copy-start | bytes 98308
  243.7 355.1 %all-reduce.10.cloned.1.call-start = ((), (), s32[]{:S(2)}) async-start(), calls=%async_computation.2 | async-start | bytes 131072 | tf_op jit(solution)/shard_map/psum | solution.py:95
  248.1 487.5 %copy-start.1 = (bf16[1,2048,3,64]{1,3,2,0:T(8,128)(2,1)S(1)}, bf16[1,2048,3,64]{1,3,2,0:T(8,128)(2,1)}, u32[]{:S(2)}) copy-start(bf16[1,2048,3,64]{1,3,2,0:T(8,128)(2,1)} %param.14) | copy-start | bytes 2359300
  248.1 487.5 %copy-start.8 = (f32[1,2048]{1,0:T(1,128)S(1)}, f32[1,2048]{1,0:T(1,128)}, u32[]{:S(2)}) copy-start(f32[1,2048]{1,0:T(1,128)} %param.13) | copy-start | bytes 24580
  534.6 205.6 %copy-start.7 = (bf16[1,64,2048]{2,1,0:T(8,128)(2,1)S(1)}, bf16[1,64,2048]{2,1,0:T(8,128)(2,1)}, u32[]{:S(2)}) copy-start(bf16[1,64,2048]{2,1,0:T(8,128)(2,1)} %param.15) | copy-start | bytes 786436
  534.6 194.7 %all-gather.5.cloned.1.call-start = ((), (), s32[]{:S(2)}) async-start(), calls=%async_computation.3 | async-start | bytes 2162688 | tf_op jit(solution)/shard_map/all_gather | solution.py:104
  600.3 452.5 %all-reduce.12.cloned.1.call-start = ((), (), s32[]{:S(2)}) async-start(), calls=%async_computation.4 | async-start | bytes 2097152 | tf_op jit(solution)/shard_map/psum | solution.py:56
  734.6 1.0 copy-start.6
  736.4 3.7 collective-permute-start
  741.7 651.7 %all-reduce.14.cloned.1.call-start = ((), (), s32[]{:S(2)}) async-start(), calls=%async_computation.5 | async-start | bytes 2097152 | tf_op jit(solution)/shard_map/psum | solution.py:56
  1054.8 40.6 %collective-permute-start.1 = (f32[128,2048]{1,0:T(8,128)S(1)}, f32[128,2048]{1,0:T(8,128)S(1)}, u32[]{:S(2)}, u32[]{:S(2)}) collective-permute-start(f32[128,2048]{1,0:T(8,128)S(1)} %bitcast_add_fusion), channel_id=1, source_target_pairs={{0,1},{1,2},{2,3},{4,5},{5,6},{6,7},{8,9},{9,10},{10,11},{12,13},{... | collective-permute-start | bytes 3145736 | tf_op jit(solution)/shard_map/ppermute | solution.py:20
  1097.2 1.0 copy-start.4
  1098.9 3.2 collective-permute-start.2
  1103.7 628.1 %all-reduce.16.cloned.1.call-start = ((), (), s32[]{:S(2)}) async-start(), calls=%async_computation.6 | async-start | bytes 2097152 | tf_op jit(solution)/shard_map/psum | solution.py:56
  1395.1 40.6 %collective-permute-start.3 = (f32[128,2048]{1,0:T(8,128)S(1)}, f32[128,2048]{1,0:T(8,128)S(1)}, u32[]{:S(2)}, u32[]{:S(2)}) collective-permute-start(f32[128,2048]{1,0:T(8,128)S(1)} %add.118), channel_id=1, source_target_pairs={{0,1},{1,2},{2,3},{4,5},{5,6},{6,7},{8,9},{9,10},{10,11},{12,13},{... | collective-permute-start | bytes 3145736 | tf_op jit(solution)/shard_map/ppermute | solution.py:20
  1435.6 1.0 copy-start.3
  1437.3 3.2 collective-permute-start.4
  1442.1 628.1 %all-reduce.18.cloned.1.call-start = ((), (), s32[]{:S(2)}) async-start(), calls=%async_computation.7 | async-start | bytes 2097152 | tf_op jit(solution)/shard_map/psum | solution.py:56
  1733.5 40.6 %collective-permute-start.5 = (f32[128,2048]{1,0:T(8,128)S(1)}, f32[128,2048]{1,0:T(8,128)S(1)}, u32[]{:S(2)}, u32[]{:S(2)}) collective-permute-start(f32[128,2048]{1,0:T(8,128)S(1)} %add.121), channel_id=1, source_target_pairs={{0,1},{1,2},{2,3},{4,5},{5,6},{6,7},{8,9},{9,10},{10,11},{12,13},{... | collective-permute-start | bytes 3145736 | tf_op jit(solution)/shard_map/ppermute | solution.py:20
  1774.0 1.0 copy-start.2
  1775.7 3.2 collective-permute-start.6
  1780.5 628.7 %all-reduce.20.cloned.1.call-start = ((), (), s32[]{:S(2)}) async-start(), calls=%async_computation.8 | async-start | bytes 2097152 | tf_op jit(solution)/shard_map/psum | solution.py:56
  2072.9 40.5 %collective-permute-start.7 = (f32[128,2048]{1,0:T(8,128)S(1)}, f32[128,2048]{1,0:T(8,128)S(1)}, u32[]{:S(2)}, u32[]{:S(2)}) collective-permute-start(f32[128,2048]{1,0:T(8,128)S(1)} %get-tuple-element.6), channel_id=1, source_target_pairs={{0,1},{1,2},{2,3},{4,5},{5,6},{6,7},{8,9},{9,10},{10,11},{12,13},{... | collective-permute-start | bytes 3145736 | tf_op jit(solution)/shard_map/ppermute | solution.py:20
  2113.4 1.0 copy-start.5
  2114.7 3.2 collective-permute-start.8
  2119.4 353.1 %reduce-scatter.6.cloned.1.call-start = ((), (), s32[]{:S(2)}) async-start(), calls=%async_computation.9 | async-start | bytes 1310720
Sparse Core Ops, SparseCore 0:
  9.0 130.9 all-gather.2
  243.8 289.1 all-reduce.21
  535.5 63.2 all-reduce.9
  600.4 128.7 all-gather.4
  741.8 310.9 all-reduce.11
  1103.8 289.5 all-reduce.13
  1442.2 289.5 all-reduce.15
  1780.6 289.4 all-reduce.17
  2119.5 289.6 all-reduce.19
  2417.5 54.9 reduce-scatter.5
where the time goes:
time: 2480 us
  waiting for transfers between devices  2030 us (82%)
  blocking collectives  248 us (10%)
  starting transfers between devices  116 us (5%)
  local copies, waits for them, and re-layouts  31.8 us (1%)
    psum x5, waiting for transfers between devices, layer_full(): return latent_state + lax.psum(update, 'blk')  1470 us
    unnamed x12, waiting for transfers between devices  208 us
    unnamed x1, blocking collectives  132 us
    all_gather x1, waiting for transfers between devices, on_device(): tower_in = lax.all_gather(start_state, 'blk', axis=1, tiled=True)  129 us
    all_gather x1, waiting for transfers between devices, on_device(): gathered = lax.all_gather(latent_queries, 'blk', axis=1, tiled=True)  128 us
    ppermute x4, starting transfers between devices, shifted(): lax.ppermute(value, axis, [(source, source + steps) for source in range(f...  113 us
    pmax x1, blocking collectives, on_device(): highest = lax.pmax(jnp.max(scores, axis=3), ('blk', 'segment'))  87.3 us
  transfers between devices with their start and end apart: 19, of which 19 were waited for; matrix products, arithmetic and copies ran while one was open for 0% of the time, Pallas kernels for 0%

commit v1 on v0

v1 whole, which is shorter than its diff:
```python
import jax
import jax.numpy as jnp
from jax import lax
from jax.experimental import pallas as pl
from jax.experimental.pallas import tpu as pltpu
from jax.sharding import PartitionSpec as P

HEADS = 16
HD = 128
LAT = 128
D = 2048
ROWS = 256
NB = 32
SR = 144
epsilon = 1e-06
masked = -1e30
MESH = pl.DeviceIdType.MESH
f32, bf16 = jnp.float32, jnp.bfloat16
NN = (((1,), (0,)), ((), ()))
NT = (((1,), (1,)), ((), ()))
TN = (((0,), (0,)), ((), ()))


def dot(a, b, dims):
    return lax.dot_general(a, b, dims, preferred_element_type=f32)


def split3(v):
    hi = v.astype(bf16).astype(f32)
    mid = (v - hi).astype(bf16).astype(f32)
    return hi, mid, v - hi - mid


def stat_rows(*rows):
    ids = lax.broadcasted_iota(jnp.int32, (16, LAT), 0)
    out = jnp.zeros((16, LAT), f32)
    for i, r in enumerate(rows):
        out = jnp.where(ids == i, jnp.broadcast_to(r, (16, LAT)), out)
    return out.astype(bf16)


def stat3(st, i):
    return st[i : i + 1] + st[i + 1 : i + 2] + st[i + 2 : i + 3]


def kernel(
    q_hbm, e_hbm, k_hbm, v_hbm, pos_ref, gain_ref, wt_hbm, wo_hbm, out_ref,
    qbuf, kb, vb, wt, wob, wot, gain2, ob, r1, r2o, r2, ebuf, xs, xb, xr, xn, ub, rb, fb,
    loc_sem, kv_send, kv_recv, w_send, w_recv, g_sem, q1_sem, q_send, q_recv,
    r1_send, r1_recv, r2_sem, r2_recv, e_send, e_recv, x_send, x_recv, u_send, u_recv,
    xr_send, xr_recv, f_send, f_recv,
):
    b = lax.axis_index("blk")
    s = lax.axis_index("segment")
    h = b // 2
    zl = b % 2
    zh = s // 2
    c = s % 2
    sib = (b, s + 1 - 2 * c)
    zpart = (b + 1 - 2 * zl, s)

    def rcopy(src, dst, ss, rs, dev):
        return pltpu.make_async_remote_copy(
            src_ref=src, dst_ref=dst, send_sem=ss, recv_sem=rs, device_id=dev, device_id_type=MESH
        )

    def plane(t):
        return lax.rem(h + t, HEADS)

    half = pl.ds(pl.multiple_of(64 * zl, 64), 64)
    loc = [
        pltpu.make_async_copy(k_hbm.at[c], kb.at[0], loc_sem.at[0]),
        pltpu.make_async_copy(v_hbm.at[c], vb.at[0], loc_sem.at[1]),
        pltpu.make_async_copy(wt_hbm, wt.at[:, half, :], loc_sem.at[2]),
        pltpu.make_async_copy(wo_hbm, wob.at[half, :], loc_sem.at[3]),
        pltpu.make_async_copy(q_hbm.at[c], qbuf.at[b], loc_sem.at[4]),
    ]
    for cp in (loc[4], loc[0], loc[1], loc[2], loc[3]):
        cp.start()

    barrier = pltpu.get_barrier_semaphore()
    for dz in range(2):
        for ds in range(4):
            if dz + ds:
                pl.semaphore_signal(
                    barrier, inc=1, device_id=(2 * h + (zl + dz) % 2, (s + ds) % 4), device_id_type=MESH
                )

    def greet(t, _):
        pl.semaphore_signal(barrier, inc=1, device_id=(plane(t) * 2 + zl, s), device_id_type=MESH)
        return 0

    lax.fori_loop(1, HEADS, greet, 0)
    pl.semaphore_wait(barrier, HEADS + 6)

    q1 = rcopy(q_hbm.at[c], qbuf.at[b], q1_sem.at[0], q1_sem.at[1], zpart)
    q1.start()
    kx = rcopy(k_hbm.at[1 - c], kb.at[1], kv_send.at[0], kv_recv.at[0], sib)
    vx = rcopy(v_hbm.at[1 - c], vb.at[1], kv_send.at[1], kv_recv.at[1], sib)
    gx = rcopy(gain_ref, gain2, g_sem.at[0], g_sem.at[1], sib)
    kx.start()
    vx.start()
    gx.start()
    loc[4].wait()
    q1.wait_recv()
    two = pl.ds(2 * h, 2)

    def q_copy(t):
        p = plane(t)
        return rcopy(qbuf.at[two], qbuf.at[two], q_send.at[t], q_recv.at[h], (p * 2 + zl, s))

    def q_start(t, _):
        q_copy(t).start()
        return 0

    lax.fori_loop(1, HEADS, q_start, 0)
    wx = rcopy(wt_hbm, wt.at[:, half, :], w_send.at[0], w_recv.at[0], zpart)
    wox = rcopy(wo_hbm, wob.at[half, :], w_send.at[1], w_recv.at[1], zpart)
    wx.start()
    wox.start()

    loc[0].wait()
    loc[1].wait()
    kx.wait_recv()
    vx.wait_recv()

    def q_wait(t, _):
        p = plane(t)
        src = pl.ds(2 * p, 2)
        rcopy(qbuf.at[src], qbuf.at[src], q_send.at[t], q_recv.at[p], (p * 2 + zl, s)).wait_recv()
        return 0

    lax.fori_loop(1, HEADS, q_wait, 0)

    def e_copy(m, t):
        p = plane(t)
        dst = p * 2 + 1 - m
        cols = pl.ds(pl.multiple_of(p * HD, HD), HD)
        return (
            e_hbm.at[m, :, cols],
            ebuf.at[b],
            m * HEADS + t,
            dst,
        )

    @pl.when(s == 0)
    def _():
        for m in range(2):
            def e_start(t, _):
                src, dst_ref, i, dst = e_copy(m, t)
                rcopy(src, dst_ref, e_send.at[i], e_recv.at[b], (dst, s)).start()
                return 0
            lax.fori_loop(1, HEADS, e_start, 0)
            src, dst_ref, i, dst = e_copy(m, 0)

            @pl.when(zl == 1 - m)
            def _():
                pltpu.make_async_copy(src, dst_ref, e_recv.at[b]).start()

            @pl.when(zl == m)
            def _():
                rcopy(src, dst_ref, e_send.at[i], e_recv.at[b], (dst, s)).start()

    base0 = (b * 4 + s) * ROWS
    base1 = (b * 4 + s + 1 - 2 * c) * ROWS
    pos = pos_ref[pl.ds(c, 1), :]
    ids = lax.broadcasted_iota(jnp.int32, (ROWS, LAT), 0)
    scale = HD ** (-0.5)

    def head_step(t, _):
        hh = plane(t + 1)
        cols = pl.ds(pl.multiple_of(hh * HD, HD), HD)
        qh = qbuf[:, :, cols].astype(f32).reshape(LAT, HD).astype(bf16)
        vis0 = ids + base0 < pos
        vis1 = ids + base1 < pos
        s0 = jnp.where(vis0, dot(kb[0, :, cols], qh, NT) * scale, masked)
        s1 = jnp.where(vis1, dot(kb[1, :, cols], qh, NT) * scale, masked)
        top = jnp.max(jnp.maximum(s0, s1), axis=0, keepdims=True)
        e0 = jnp.where(vis0, jnp.exp(s0 - top), 0.0)
        e1 = jnp.where(vis1, jnp.exp(s1 - top), 0.0)
        total = jnp.sum(e0 + e1, axis=0, keepdims=True)
        o = dot(vb[0, :, cols], e0.astype(bf16), TN) + dot(vb[1, :, cols], e1.astype(bf16), TN)
        ob[hh, 0:HD, :] = o.astype(bf16)
        ob[hh, HD:SR, :] = stat_rows(*split3(top), *split3(total))

        @pl.when(t < HEADS - 1)
        def _():
            rcopy(ob.at[hh], r1.at[h], r1_send.at[hh], r1_recv.at[h], (hh * 2 + zl, s)).start()

        return 0

    lax.fori_loop(0, HEADS, head_step, 0)

    def r1_wait(t, _):
        p = plane(t)
        rcopy(ob.at[p], r1.at[p], r1_send.at[p], r1_recv.at[p], (p * 2 + zl, s)).wait_recv()
        return 0

    lax.fori_loop(1, HEADS, r1_wait, 0)
    r1[h] = ob[h]

    def combine(buf, n):
        st = [buf[i, HD:SR, :].astype(f32) for i in range(n)]
        tops = [stat3(v, 0) for v in st]
        top = tops[0]
        for v in tops[1:]:
            top = jnp.maximum(top, v)
        total = jnp.zeros((1, LAT), f32)
        acc = jnp.zeros((HD, LAT), f32)
        for i in range(n):
            w = jnp.exp(tops[i] - top)
            total = total + w * stat3(st[i], 3)
            acc = acc + w * buf[i, 0:HD, :].astype(f32)
        return acc, top, total

    acc, top, total = combine(r1, HEADS)
    r2o[0:HD, :] = acc.astype(bf16)
    r2o[HD:SR, :] = stat_rows(*split3(top), *split3(total))
    z = zh * 2 + zl
    r2_home = (s == 0) & (zl == 1 - c)
    r2_dst = (2 * h + 1 - c, 0)

    @pl.when(r2_home)
    def _():
        pltpu.make_async_copy(r2o, r2.at[z], r2_recv.at[z]).start()

    @pl.when(jnp.logical_not(r2_home))
    def _():
        rcopy(r2o, r2.at[z], r2_sem.at[0], r2_recv.at[z], r2_dst).start()

    loc[2].wait()
    loc[3].wait()
    wx.wait_recv()
    wox.wait_recv()
    for j in range(HEADS):
        wot[j] = wob[:, j * HD : (j + 1) * HD].T
    gx.wait_recv()
    my_cols = pl.ds(pl.multiple_of(h * HD, HD), HD)

    def column(ref):
        return jnp.broadcast_to(ref[:, my_cols], (HD, LAT)).T

    def pack_x(x, gain):
        xs[0:HD, :] = (x * gain).astype(bf16)
        xs[HD:SR, :] = stat_rows(*split3(jnp.sum(x * x, axis=0, keepdims=True)))

    @pl.when(c == 0)
    def _():
        @pl.when(s == 0)
        def _():
            def e_wait(i, _):
                pltpu.make_async_copy(e_hbm.at[0, :, pl.ds(0, HD)], ebuf.at[i], e_recv.at[i]).wait()
                return 0

            lax.fori_loop(0, NB, e_wait, 0)
            for i in range(4):
                pltpu.make_async_copy(r2o, r2.at[i], r2_recv.at[i]).wait()
            acc, top, total = combine(r2, 4)
            emb = ebuf[...].astype(f32).reshape(LAT, HD).T
            xr[...] = emb + acc / total

        @pl.when(s == 2)
        def _():
            pltpu.make_async_copy(xn, xr, xr_recv.at[0]).wait()

        pack_x(xr[...], column(gain_ref))

        def x_start(t, _):
            p = plane(t)
            rcopy(xs, xb.at[h], x_send.at[t], x_recv.at[h], (p * 2 + zl, s)).start()
            return 0

        lax.fori_loop(1, HEADS, x_start, 0)
        pltpu.make_async_copy(xs, xb.at[h], x_recv.at[h]).start()

    def x_wait(i, _):
        pltpu.make_async_copy(xs, xb.at[i], x_recv.at[i]).wait()
        return 0

    lax.fori_loop(0, HEADS, x_wait, 0)

    wfull = wt[...].reshape(3 * HD, D)
    qkv = jnp.zeros((3 * HD, LAT), f32)
    ss = jnp.zeros((1, LAT), f32)
    for j in range(HEADS // 2):
        pair = jnp.concatenate([xb[2 * j, 0:HD, :], xb[2 * j + 1, 0:HD, :]], axis=0)
        qkv = qkv + dot(wfull[:, 2 * j * HD : (2 * j + 2) * HD], pair, NN)
    for j in range(HEADS):
        ss = ss + stat3(xb[j, HD:SR, :].astype(f32), 0)
    factor = lax.rsqrt(ss * (1.0 / D) + epsilon)
    qkv = (qkv * factor).astype(bf16)
    qt, kt, vt = qkv[0:HD], qkv[HD : 2 * HD], qkv[2 * HD :]
    sc = dot(kt, qt, TN) * scale
    jj = lax.broadcasted_iota(jnp.int32, (LAT, LAT), 0)
    ii = lax.broadcasted_iota(jnp.int32, (LAT, LAT), 1)
    sc = jnp.where(jj <= ii, sc, masked)
    e = jnp.exp(sc - jnp.max(sc, axis=0, keepdims=True))
    soft = (e / jnp.sum(e, axis=0, keepdims=True)).astype(bf16)
    att = dot(vt, soft, NN).astype(bf16)

    def u_step(t, _):
        p = plane(t + 1)
        ub[p] = dot(wot[p], att, NN).astype(bf16)

        @pl.when(t < HEADS - 1)
        def _():
            rcopy(ub.at[p], rb.at[h], u_send.at[p], u_recv.at[h], (p * 2 + zl, s)).start()

        return 0

    lax.fori_loop(0, HEADS, u_step, 0)

    @pl.when(c == 1)
    def _():
        pltpu.make_async_copy(xn, xr, xr_recv.at[0]).wait()

    def u_wait(t, _):
        p = plane(t)
        rcopy(ub.at[p], rb.at[p], u_send.at[p], u_recv.at[p], (p * 2 + zl, s)).wait_recv()
        return 0

    lax.fori_loop(1, HEADS, u_wait, 0)
    rb[h] = ub[h]
    x = xr[...]
    for j in range(HEADS):
        x = x + rb[j].astype(f32)
    xn[...] = x

    @pl.when(c == 0)
    def _():
        def x_drain(t, _):
            pltpu.make_async_copy(xs, xb.at[0], x_send.at[t]).wait()
            return 0

        lax.fori_loop(1, HEADS, x_drain, 0)
        pack_x(xn[...], column(gain2))

        def x_next(t, _):
            p = plane(t)
            rcopy(xs, xb.at[h], x_send.at[t], x_recv.at[h], (p * 2 + zl, s + 1)).start()
            return 0

        lax.fori_loop(0, HEADS, x_next, 0)
        up = rcopy(xn, xr, xr_send.at[0], xr_recv.at[0], sib)
        up.start()

        def x_drain2(t, _):
            pltpu.make_async_copy(xs, xb.at[0], x_send.at[t]).wait()
            return 0

        lax.fori_loop(0, HEADS, x_drain2, 0)
        up.wait_send()

    @pl.when(s == 1)
    def _():
        up = rcopy(xn, xr, xr_send.at[0], xr_recv.at[0], (b + 1 - 2 * zl, 2))
        up.start()
        up.wait_send()

    seg = h // 4
    f_cols = pl.ds(pl.multiple_of(lax.rem(h, 4) * HD, HD), HD)

    @pl.when(s == 3)
    def _():
        fb[...] = xn[...].T.reshape(NB, 4, HD)

        def f_start(i, _):
            away = jnp.logical_or(i != b, seg != s)
            dst = out_ref.at[zl, :, f_cols]
            sem = f_recv.at[zl * 4 + lax.rem(h, 4)]

            @pl.when(away)
            def _():
                rcopy(fb.at[i], dst, f_send.at[i], sem, (i, seg)).start()

            @pl.when(jnp.logical_not(away))
            def _():
                pltpu.make_async_copy(fb.at[i], dst, sem).start()

            return 0

        lax.fori_loop(0, NB, f_start, 0)

        def f_drain(i, _):
            @pl.when(jnp.logical_or(i != b, seg != s))
            def _():
                pltpu.make_async_copy(fb.at[i], fb.at[i], f_send.at[i]).wait()

            return 0

        lax.fori_loop(0, NB, f_drain, 0)

    q1.wait_send()
    kx.wait_send()
    vx.wait_send()
    gx.wait_send()
    wx.wait_send()
    wox.wait_send()

    def drain(t, _):
        q_copy(t).wait_send()
        p = plane(t)
        rcopy(ob.at[p], r1.at[h], r1_send.at[p], r1_recv.at[h], (p * 2 + zl, s)).wait_send()
        rcopy(ub.at[p], rb.at[h], u_send.at[p], u_recv.at[h], (p * 2 + zl, s)).wait_send()
        return 0

    lax.fori_loop(1, HEADS, drain, 0)

    @pl.when(jnp.logical_not(r2_home))
    def _():
        rcopy(r2o, r2.at[z], r2_sem.at[0], r2_recv.at[z], r2_dst).wait_send()

    @pl.when(s == 0)
    def _():
        for m in range(2):
            def e_drain(t, _):
                src, dst_ref, i, dst = e_copy(m, t)
                pltpu.make_async_copy(src, dst_ref, e_send.at[i]).wait()
                return 0

            lax.fori_loop(1, HEADS, e_drain, 0)

            @pl.when(zl == m)
            def _():
                src, dst_ref, i, dst = e_copy(m, 0)
                pltpu.make_async_copy(src, dst_ref, e_send.at[i]).wait()

    for m in range(2):
        for i in range(4):
            pltpu.make_async_copy(
                fb.at[0], out_ref.at[m, :, i * HD : (i + 1) * HD], f_recv.at[m * 4 + i]
            ).wait()


def on_device(
    latent_queries, latent_embed, history_keys, history_values, latent_pos, norm_gain, w_qkv, w_out
):
    wt = jnp.transpose(w_qkv[0], (1, 2, 0))
    hbm = pl.BlockSpec(memory_space=pl.ANY)
    vmem = pl.BlockSpec(memory_space=pltpu.VMEM)
    dma = pltpu.SemaphoreType.DMA
    return pl.pallas_call(
        kernel,
        out_shape=jax.ShapeDtypeStruct((2, 4, 512), f32),
        in_specs=[hbm, hbm, hbm, hbm, vmem, vmem, hbm, hbm],
        out_specs=vmem,
        scratch_shapes=[
            pltpu.VMEM((NB, 4, D), bf16),
            pltpu.VMEM((2, ROWS, D), bf16),
            pltpu.VMEM((2, ROWS, D), bf16),
            pltpu.VMEM((3, HD, D), bf16),
            pltpu.VMEM((HD, D), bf16),
            pltpu.VMEM((HEADS, HD, HD), bf16),
            pltpu.VMEM((1, D), f32),
            pltpu.VMEM((HEADS, SR, LAT), bf16),
            pltpu.VMEM((HEADS, SR, LAT), bf16),
            pltpu.VMEM((SR, LAT), bf16),
            pltpu.VMEM((4, SR, LAT), bf16),
            pltpu.VMEM((NB, 4, HD), bf16),
            pltpu.VMEM((SR, LAT), bf16),
            pltpu.VMEM((HEADS, SR, LAT), bf16),
            pltpu.VMEM((HD, LAT), f32),
            pltpu.VMEM((HD, LAT), f32),
            pltpu.VMEM((HEADS, HD, LAT), bf16),
            pltpu.VMEM((HEADS, HD, LAT), bf16),
            pltpu.VMEM((NB, 4, HD), f32),
            dma((5,)), dma((2,)), dma((2,)), dma((2,)), dma((2,)), dma((2,)), dma((2,)),
            dma((HEADS,)), dma((HEADS,)), dma((HEADS,)), dma((HEADS,)), dma((1,)), dma((4,)),
            dma((2 * HEADS,)), dma((NB,)), dma((HEADS,)), dma((HEADS,)), dma((HEADS,)), dma((HEADS,)),
            dma((1,)), dma((1,)), dma((NB,)), dma((8,)),
        ],
        compiler_params=pltpu.CompilerParams(
            collective_id=0, has_side_effects=True, vmem_limit_bytes=67043328
        ),
        name="ar_step",
    )(latent_queries, latent_embed, history_keys, history_values, latent_pos, norm_gain, wt, w_out[0])


def solution(mesh):
    return jax.shard_map(
        on_device,
        mesh=mesh,
        in_specs=(
            P(None, "blk", None),
            P(None, "blk", None),
            P(None, ("blk", "segment"), None),
            P(None, ("blk", "segment"), None),
            P(),
            P("segment", None),
            P("segment", None, None, "blk"),
            P("segment", "blk", None),
        ),
        out_specs=P(None, "blk", "segment"),
        check_vma=False,
    )
```

time: 2480 us -> 111 us (0.04)
  waiting for transfers between devices: 2030 us -> 0 us
  blocking collectives: 248 us -> 0 us
  starting transfers between devices: 116 us -> 0 us
  Pallas kernels: 0 us -> 109 us
  local copies, waits for them, and re-layouts: 31.8 us -> 1.32 us
    psum x6 -> x0, waiting for transfers between devices: 1500 us -> none  [the longest x5 1470 us: layer_full(): return latent_state + lax.psum(update, 'blk')]
    all_gather x2 -> x0, waiting for transfers between devices: 257 us -> none  [the longest x1 129 us: on_device(): tower_in = lax.all_gather(start_state, 'blk', axis=1, tiled=True)]
    unnamed x12 -> x0, waiting for transfers between devices: 208 us -> none
    unnamed x1 -> x0, blocking collectives: 132 us -> none
    ppermute x9 -> x0, starting transfers between devices: 116 us -> none  [the longest x4 113 us: shifted(): lax.ppermute(value, axis, [(source, source + steps) for source in range(f...]
    pallas_call x0 -> x1, Pallas kernels: none -> 109 us  [on_device(): pl.pallas_call(kernel, out_shape=jax.ShapeDtypeStruct((2, 4, 512), f32),...]
    pmax x1 -> x0, blocking collectives: 87.3 us -> none  [on_device(): highest = lax.pmax(jnp.max(scores, axis=3), ('blk', 'segment'))]
    ppermute x9 -> x0, waiting for transfers between devices: 62.8 us -> none  [the longest x4 49.5 us: shifted(): lax.ppermute(value, axis, [(source, source + steps) for source in range(f...]
  transfers between devices with their start and end apart: 19 -> 0, of which waited for: 19 -> 0; matrix products, arithmetic and copies ran while one was open for 0% -> 0% of each run, Pallas kernels for 0% -> 0%
where the time goes in v1:
time: 111 us; the launch traced here: 110 us
  Pallas kernels  109 us (98%)
  local copies, waits for them, and re-layouts  1.32 us (1%)
    pallas_call x1, Pallas kernels, on_device(): pl.pallas_call(kernel, out_shape=jax.ShapeDtypeStruct((2, 4, 512), f32),...  109 us

profile of v1, /device:TPU:1, one launch (start us, length us, event | category | flops | bytes accessed | tf_op | source)
XLA Modules:
  0.0 110.5 jit_solution(15484008518641275772)
XLA Ops:
  0.0 109.1 %ar_step.1 = f32[2,4,512]{2,1,0:T(4,128)} custom-call(bf16[2,4,2048]{2,1,0:T(4,128)(2,1)} %q_hbm.1, bf16[2,4,2048]{2,1,0:T(4,128)(2,1)} %e_hbm.1, bf16[2,256,2048]{2,1,0:T(8,128)(2,1)} %k_hbm.1, bf16[2,256,2048]{2,1,0:T(8,128)(2,1)} %v_hbm.1, s32[2,128]{1,0:T(2,128)} %pos_ref.1, f32[1,2048]{1,0:T(1,128)} %gain_ref.1, bf16[3,64,2048]{2,1,0:T(8,128)(2,1)} %bitcast.4, ...), custom_call_target="tpu_custom_call" | custom-call | tf_op jit(solution)/shard_map/ar_step/pallas_call | solution.py:442
  109.1 1.3 %copy.10 = f32[2,4,512]{2,1,0:T(4,128)} copy(f32[2,4,512]{2,1,0:T(4,128)} %ar_step.1) | data formatting | bytes 32768

commit v2 on v1

--- a/solution.py
+++ b/solution.py
@@ -19,6 +19,10 @@
 NN = (((1,), (0,)), ((), ()))
 NT = (((1,), (1,)), ((), ()))
 TN = (((0,), (0,)), ((), ()))
+FAR = sorted(
+    ((dx, dy) for dx in range(4) for dy in range(4) if dx or dy),
+    key=lambda o: -min(o[0], 4 - o[0]) - min(o[1], 4 - o[1]),
+)
 
 
 def dot(a, b, dims):
@@ -45,7 +49,7 @@
 
 def kernel(
     q_hbm, e_hbm, k_hbm, v_hbm, pos_ref, gain_ref, wt_hbm, wo_hbm, out_ref,
-    qbuf, kb, vb, wt, wob, wot, gain2, ob, r1, r2o, r2, ebuf, xs, xb, xr, xn, ub, rb, fb,
+    qbuf, kb, vb, vts, wt, wob, wot, gain2, ob, r1, r2o, r2, ebuf, xs, xb, xr, xn, ub, rb, fb,
     loc_sem, kv_send, kv_recv, w_send, w_recv, g_sem, q1_sem, q_send, q_recv,
     r1_send, r1_recv, r2_sem, r2_recv, e_send, e_recv, x_send, x_recv, u_send, u_recv,
     xr_send, xr_recv, f_send, f_recv,
@@ -64,8 +68,13 @@
             src_ref=src, dst_ref=dst, send_sem=ss, recv_sem=rs, device_id=dev, device_id_type=MESH
         )
 
-    def plane(t):
-        return lax.rem(h + t, HEADS)
+    hx, hy = h // 4, lax.rem(h, 4)
+
+    def chip(dx, dy):
+        return lax.rem(hx + dx, 4) * 4 + lax.rem(hy + dy, 4)
+
+    far = [chip(*o) for o in FAR]
+    near = [h] + far[::-1]
 
     half = pl.ds(pl.multiple_of(64 * zl, 64), 64)
     loc = [
@@ -86,54 +95,52 @@
                     barrier, inc=1, device_id=(2 * h + (zl + dz) % 2, (s + ds) % 4), device_id_type=MESH
                 )
 
-    def greet(t, _):
-        pl.semaphore_signal(barrier, inc=1, device_id=(plane(t) * 2 + zl, s), device_id_type=MESH)
-        return 0
-
-    lax.fori_loop(1, HEADS, greet, 0)
+    for p in far:
+        pl.semaphore_signal(barrier, inc=1, device_id=(p * 2 + zl, s), device_id_type=MESH)
     pl.semaphore_wait(barrier, HEADS + 6)
 
-    q1 = rcopy(q_hbm.at[c], qbuf.at[b], q1_sem.at[0], q1_sem.at[1], zpart)
+    other = b + 1 - 2 * zl
+    q1 = rcopy(q_hbm.at[c], qbuf.at[b], q1_sem.at[0], q_recv.at[b], zpart)
     q1.start()
+    wx = rcopy(wt_hbm, wt.at[:, half, :], w_send.at[0], w_recv.at[0], zpart)
+    wx.start()
+    sent = []
+
+    def go(cp):
+        cp.start()
+        sent.append(cp)
+
+    for i, p in enumerate(far):
+        go(rcopy(q_hbm.at[c], qbuf.at[b], q_send.at[i], q_recv.at[b], (p * 2 + zl, s)))
     kx = rcopy(k_hbm.at[1 - c], kb.at[1], kv_send.at[0], kv_recv.at[0], sib)
     vx = rcopy(v_hbm.at[1 - c], vb.at[1], kv_send.at[1], kv_recv.at[1], sib)
     gx = rcopy(gain_ref, gain2, g_sem.at[0], g_sem.at[1], sib)
     kx.start()
     vx.start()
     gx.start()
+
+    def q_wait(i):
+        pltpu.make_async_copy(q_hbm.at[c], qbuf.at[i], q_recv.at[i]).wait()
+
+    q_wait(other)
+    for i, p in enumerate(far):
+        go(rcopy(qbuf.at[other], qbuf.at[other], q_send.at[15 + i], q_recv.at[other], (p * 2 + zl, s)))
+
+    loc[1].wait()
+    for j in range(HEADS):
+        vts[j, :, 0:ROWS] = vb[0, :, j * HD : (j + 1) * HD].T
+    vx.wait_recv()
+    for j in range(HEADS):
+        vts[j, :, ROWS : 2 * ROWS] = vb[1, :, j * HD : (j + 1) * HD].T
+    loc[0].wait()
+    kx.wait_recv()
     loc[4].wait()
-    q1.wait_recv()
-    two = pl.ds(2 * h, 2)
-
-    def q_copy(t):
-        p = plane(t)
-        return rcopy(qbuf.at[two], qbuf.at[two], q_send.at[t], q_recv.at[h], (p * 2 + zl, s))
-
-    def q_start(t, _):
-        q_copy(t).start()
-        return 0
-
-    lax.fori_loop(1, HEADS, q_start, 0)
-    wx = rcopy(wt_hbm, wt.at[:, half, :], w_send.at[0], w_recv.at[0], zpart)
-    wox = rcopy(wo_hbm, wob.at[half, :], w_send.at[1], w_recv.at[1], zpart)
-    wx.start()
-    wox.start()
-
-    loc[0].wait()
-    loc[1].wait()
-    kx.wait_recv()
-    vx.wait_recv()
-
-    def q_wait(t, _):
-        p = plane(t)
-        src = pl.ds(2 * p, 2)
-        rcopy(qbuf.at[src], qbuf.at[src], q_send.at[t], q_recv.at[p], (p * 2 + zl, s)).wait_recv()
-        return 0
-
-    lax.fori_loop(1, HEADS, q_wait, 0)
+    for p in far:
+        q_wait(2 * p + zl)
+        q_wait(2 * p + 1 - zl)
 
     def e_copy(m, t):
-        p = plane(t)
+        p = lax.rem(h + t, HEADS)
         dst = p * 2 + 1 - m
         cols = pl.ds(pl.multiple_of(p * HD, HD), HD)
         return (
@@ -167,36 +174,37 @@
     ids = lax.broadcasted_iota(jnp.int32, (ROWS, LAT), 0)
     scale = HD ** (-0.5)
 
-    def head_step(t, _):
-        hh = plane(t + 1)
+    ids1 = ids + base1
+    ids0 = ids + base0
+
+    def scores(hh):
         cols = pl.ds(pl.multiple_of(hh * HD, HD), HD)
         qh = qbuf[:, :, cols].astype(f32).reshape(LAT, HD).astype(bf16)
-        vis0 = ids + base0 < pos
-        vis1 = ids + base1 < pos
-        s0 = jnp.where(vis0, dot(kb[0, :, cols], qh, NT) * scale, masked)
-        s1 = jnp.where(vis1, dot(kb[1, :, cols], qh, NT) * scale, masked)
-        top = jnp.max(jnp.maximum(s0, s1), axis=0, keepdims=True)
-        e0 = jnp.where(vis0, jnp.exp(s0 - top), 0.0)
-        e1 = jnp.where(vis1, jnp.exp(s1 - top), 0.0)
+        s0 = jnp.where(ids0 < pos, dot(kb[0, :, cols], qh, NT) * scale, masked)
+        s1 = jnp.where(ids1 < pos, dot(kb[1, :, cols], qh, NT) * scale, masked)
+        return s0, s1
+
+    def weigh(s0, s1):
+        top = jnp.maximum(jnp.max(jnp.maximum(s0, s1), axis=0, keepdims=True), 0.1 * masked)
+        e0, e1 = jnp.exp(s0 - top), jnp.exp(s1 - top)
         total = jnp.sum(e0 + e1, axis=0, keepdims=True)
-        o = dot(vb[0, :, cols], e0.astype(bf16), TN) + dot(vb[1, :, cols], e1.astype(bf16), TN)
-        ob[hh, 0:HD, :] = o.astype(bf16)
-        ob[hh, HD:SR, :] = stat_rows(*split3(top), *split3(total))
-
-        @pl.when(t < HEADS - 1)
-        def _():
-            rcopy(ob.at[hh], r1.at[h], r1_send.at[hh], r1_recv.at[h], (hh * 2 + zl, s)).start()
-
-        return 0
-
-    lax.fori_loop(0, HEADS, head_step, 0)
-
-    def r1_wait(t, _):
-        p = plane(t)
-        rcopy(ob.at[p], r1.at[p], r1_send.at[p], r1_recv.at[p], (p * 2 + zl, s)).wait_recv()
-        return 0
-
-    lax.fori_loop(1, HEADS, r1_wait, 0)
+        return top, total, jnp.concatenate([e0.astype(bf16), e1.astype(bf16)], axis=0)
+
+    order = far + [h]
+    for g in range(0, HEADS, 2):
+        group = order[g : g + 2]
+        ss = [scores(hh) for hh in group]
+        ws = [weigh(*v) for v in ss]
+        for hh, (top, total, e) in zip(group, ws):
+            ob[hh, 0:HD, :] = dot(vts[hh], e, NN).astype(bf16)
+            ob[hh, HD:SR, :] = stat_rows(*split3(top), *split3(total))
+        for i in range(g, g + 2):
+            if i < HEADS - 1:
+                hh = order[i]
+                go(rcopy(ob.at[hh], r1.at[h], r1_send.at[i], r1_recv.at[h], (hh * 2 + zl, s)))
+
+    for p in near[1:]:
+        pltpu.make_async_copy(r2o, r1.at[p], r1_recv.at[p]).wait()
     r1[h] = ob[h]
 
     def combine(buf, n):
@@ -228,12 +236,9 @@
     def _():
         rcopy(r2o, r2.at[z], r2_sem.at[0], r2_recv.at[z], r2_dst).start()
 
-    loc[2].wait()
-    loc[3].wait()
-    wx.wait_recv()
-    wox.wait_recv()
-    for j in range(HEADS):
-        wot[j] = wob[:, j * HD : (j + 1) * HD].T
+    wox = rcopy(wo_hbm, wob.at[half, :], w_send.at[1], w_recv.at[1], zpart)
+    wox.start()
+
     gx.wait_recv()
     my_cols = pl.ds(pl.multiple_of(h * HD, HD), HD)
 
@@ -265,28 +270,27 @@
 
         pack_x(xr[...], column(gain_ref))
 
-        def x_start(t, _):
-            p = plane(t)
-            rcopy(xs, xb.at[h], x_send.at[t], x_recv.at[h], (p * 2 + zl, s)).start()
-            return 0
-
-        lax.fori_loop(1, HEADS, x_start, 0)
+        for i, p in enumerate(far):
+            rcopy(xs, xb.at[h], x_send.at[i], x_recv.at[h], (p * 2 + zl, s)).start()
         pltpu.make_async_copy(xs, xb.at[h], x_recv.at[h]).start()
 
-    def x_wait(i, _):
-        pltpu.make_async_copy(xs, xb.at[i], x_recv.at[i]).wait()
-        return 0
-
-    lax.fori_loop(0, HEADS, x_wait, 0)
-
-    wfull = wt[...].reshape(3 * HD, D)
+    loc[2].wait()
+    wx.wait_recv()
     qkv = jnp.zeros((3 * HD, LAT), f32)
     ss = jnp.zeros((1, LAT), f32)
-    for j in range(HEADS // 2):
-        pair = jnp.concatenate([xb[2 * j, 0:HD, :], xb[2 * j + 1, 0:HD, :]], axis=0)
-        qkv = qkv + dot(wfull[:, 2 * j * HD : (2 * j + 2) * HD], pair, NN)
+    for j in range(0, HEADS, 2):
+        pair = near[j : j + 2]
+        for p in pair:
+            pltpu.make_async_copy(xs, xb.at[p], x_recv.at[p]).wait()
+        w2 = [wt[:, :, pl.ds(pl.multiple_of(p * HD, HD), HD)].reshape(3 * HD, HD) for p in pair]
+        x2 = [xb[p, 0:HD, :] for p in pair]
+        qkv = qkv + dot(jnp.concatenate(w2, axis=1), jnp.concatenate(x2, axis=0), NN)
+        for p in pair:
+            ss = ss + stat3(xb[p, HD:SR, :].astype(f32), 0)
+    loc[3].wait()
+    wox.wait_recv()
     for j in range(HEADS):
-        ss = ss + stat3(xb[j, HD:SR, :].astype(f32), 0)
+        wot[j] = wob[:, j * HD : (j + 1) * HD].T
     factor = lax.rsqrt(ss * (1.0 / D) + epsilon)
     qkv = (qkv * factor).astype(bf16)
     qt, kt, vt = qkv[0:HD], qkv[HD : 2 * HD], qkv[2 * HD :]
@@ -298,57 +302,36 @@
     soft = (e / jnp.sum(e, axis=0, keepdims=True)).astype(bf16)
     att = dot(vt, soft, NN).astype(bf16)
 
-    def u_step(t, _):
-        p = plane(t + 1)
-        ub[p] = dot(wot[p], att, NN).astype(bf16)
-
-        @pl.when(t < HEADS - 1)
-        def _():
-            rcopy(ub.at[p], rb.at[h], u_send.at[p], u_recv.at[h], (p * 2 + zl, s)).start()
-
-        return 0
-
-    lax.fori_loop(0, HEADS, u_step, 0)
+    for g in range(0, HEADS - 1, 5):
+        us = [dot(wot[p], att, NN).astype(bf16) for p in far[g : g + 5]]
+        for p, u in zip(far[g : g + 5], us):
+            ub[p] = u
+        for i, p in enumerate(far[g : g + 5], g):
+            go(rcopy(ub.at[p], rb.at[h], u_send.at[i], u_recv.at[h], (p * 2 + zl, s)))
+    own = dot(wot[h], att, NN)
 
     @pl.when(c == 1)
     def _():
         pltpu.make_async_copy(xn, xr, xr_recv.at[0]).wait()
 
-    def u_wait(t, _):
-        p = plane(t)
-        rcopy(ub.at[p], rb.at[p], u_send.at[p], u_recv.at[p], (p * 2 + zl, s)).wait_recv()
-        return 0
-
-    lax.fori_loop(1, HEADS, u_wait, 0)
-    rb[h] = ub[h]
-    x = xr[...]
-    for j in range(HEADS):
-        x = x + rb[j].astype(f32)
+    x = xr[...] + own
+    for p in near[1:]:
+        pltpu.make_async_copy(ub.at[p], rb.at[p], u_recv.at[p]).wait()
+        x = x + rb[p].astype(f32)
     xn[...] = x
 
     @pl.when(c == 0)
     def _():
-        def x_drain(t, _):
-            pltpu.make_async_copy(xs, xb.at[0], x_send.at[t]).wait()
-            return 0
-
-        lax.fori_loop(1, HEADS, x_drain, 0)
+        for i in range(HEADS - 1):
+            pltpu.make_async_copy(xs, xb.at[0], x_send.at[i]).wait()
         pack_x(xn[...], column(gain2))
 
-        def x_next(t, _):
-            p = plane(t)
-            rcopy(xs, xb.at[h], x_send.at[t], x_recv.at[h], (p * 2 + zl, s + 1)).start()
-            return 0
-
-        lax.fori_loop(0, HEADS, x_next, 0)
+        for i, p in enumerate(far + [h]):
+            rcopy(xs, xb.at[h], x_send.at[i], x_recv.at[h], (p * 2 + zl, s + 1)).start()
         up = rcopy(xn, xr, xr_send.at[0], xr_recv.at[0], sib)
         up.start()
-
-        def x_drain2(t, _):
-            pltpu.make_async_copy(xs, xb.at[0], x_send.at[t]).wait()
-            return 0
-
-        lax.fori_loop(0, HEADS, x_drain2, 0)
+        for i in range(HEADS):
+            pltpu.make_async_copy(xs, xb.at[0], x_send.at[i]).wait()
         up.wait_send()
 
     @pl.when(s == 1)
@@ -364,31 +347,27 @@
     def _():
         fb[...] = xn[...].T.reshape(NB, 4, HD)
 
-        def f_start(i, _):
-            away = jnp.logical_or(i != b, seg != s)
-            dst = out_ref.at[zl, :, f_cols]
-            sem = f_recv.at[zl * 4 + lax.rem(h, 4)]
-
-            @pl.when(away)
-            def _():
-                rcopy(fb.at[i], dst, f_send.at[i], sem, (i, seg)).start()
-
-            @pl.when(jnp.logical_not(away))
-            def _():
-                pltpu.make_async_copy(fb.at[i], dst, sem).start()
-
-            return 0
-
-        lax.fori_loop(0, NB, f_start, 0)
-
-        def f_drain(i, _):
-            @pl.when(jnp.logical_or(i != b, seg != s))
-            def _():
-                pltpu.make_async_copy(fb.at[i], fb.at[i], f_send.at[i]).wait()
-
-            return 0
-
-        lax.fori_loop(0, NB, f_drain, 0)
+        dst = out_ref.at[zl, :, f_cols]
+        sem = f_recv.at[zl * 4 + lax.rem(h, 4)]
+        for i, p in enumerate(far):
+            for dz in range(2):
+                rcopy(fb.at[2 * p + dz], dst, f_send.at[2 * i + dz], sem, (2 * p + dz, seg)).start()
+        rcopy(fb.at[other], dst, f_send.at[30], sem, (other, seg)).start()
+
+        @pl.when(seg != s)
+        def _():
+            rcopy(fb.at[b], dst, f_send.at[31], sem, (b, seg)).start()
+
+        @pl.when(seg == s)
+        def _():
+            pltpu.make_async_copy(fb.at[b], dst, sem).start()
+
+        for i in range(31):
+            pltpu.make_async_copy(fb.at[i], fb.at[i], f_send.at[i]).wait()
+
+        @pl.when(seg != s)
+        def _():
+            pltpu.make_async_copy(fb.at[0], fb.at[0], f_send.at[31]).wait()
 
     q1.wait_send()
     kx.wait_send()
@@ -397,14 +376,8 @@
     wx.wait_send()
     wox.wait_send()
 
-    def drain(t, _):
-        q_copy(t).wait_send()
-        p = plane(t)
-        rcopy(ob.at[p], r1.at[h], r1_send.at[p], r1_recv.at[h], (p * 2 + zl, s)).wait_send()
-        rcopy(ub.at[p], rb.at[h], u_send.at[p], u_recv.at[h], (p * 2 + zl, s)).wait_send()
-        return 0
-
-    lax.fori_loop(1, HEADS, drain, 0)
+    for cp in sent:
+        cp.wait_send()
 
     @pl.when(jnp.logical_not(r2_home))
     def _():
@@ -448,6 +421,7 @@
             pltpu.VMEM((NB, 4, D), bf16),
             pltpu.VMEM((2, ROWS, D), bf16),
             pltpu.VMEM((2, ROWS, D), bf16),
+            pltpu.VMEM((HEADS, HD, 2 * ROWS), bf16),
             pltpu.VMEM((3, HD, D), bf16),
             pltpu.VMEM((HD, D), bf16),
             pltpu.VMEM((HEADS, HD, HD), bf16),
@@ -465,7 +439,7 @@
             pltpu.VMEM((HEADS, HD, LAT), bf16),
             pltpu.VMEM((NB, 4, HD), f32),
             dma((5,)), dma((2,)), dma((2,)), dma((2,)), dma((2,)), dma((2,)), dma((2,)),
-            dma((HEADS,)), dma((HEADS,)), dma((HEADS,)), dma((HEADS,)), dma((1,)), dma((4,)),
+            dma((NB,)), dma((NB,)), dma((HEADS,)), dma((HEADS,)), dma((1,)), dma((4,)),
             dma((2 * HEADS,)), dma((NB,)), dma((HEADS,)), dma((HEADS,)), dma((HEADS,)), dma((HEADS,)),
             dma((1,)), dma((1,)), dma((NB,)), dma((8,)),
         ],

time: 111 us -> 99.4 us (0.90)
  Pallas kernels: 109 us -> 97.8 us
    pallas_call x1, Pallas kernels: 109 us -> 97.8 us  [on_device(): pl.pallas_call(kernel, out_shape=jax.ShapeDtypeStruct((2, 4, 512), f32),...]
where the time goes in v2:
time: 99.4 us; the launch traced here: 99.1 us
  Pallas kernels  97.8 us (98%)
  local copies, waits for them, and re-layouts  1.32 us (1%)
    pallas_call x1, Pallas kernels, on_device(): pl.pallas_call(kernel, out_shape=jax.ShapeDtypeStruct((2, 4, 512), f32),...  97.8 us

profile of v2, /device:TPU:1, one launch (start us, length us, event | category | flops | bytes accessed | tf_op | source)
XLA Modules:
  0.0 99.1 jit_solution(9149477901550905475)
XLA Ops:
  0.0 97.8 %ar_step.1 = f32[2,4,512]{2,1,0:T(4,128)} custom-call(bf16[2,4,2048]{2,1,0:T(4,128)(2,1)} %q_hbm.1, bf16[2,4,2048]{2,1,0:T(4,128)(2,1)} %e_hbm.1, bf16[2,256,2048]{2,1,0:T(8,128)(2,1)} %k_hbm.1, bf16[2,256,2048]{2,1,0:T(8,128)(2,1)} %v_hbm.1, s32[2,128]{1,0:T(2,128)} %pos_ref.1, f32[1,2048]{1,0:T(1,128)} %gain_ref.1, bf16[3,64,2048]{2,1,0:T(8,128)(2,1)} %bitcast.4, ...), custom_call_target="tpu_custom_call" | custom-call | tf_op jit(solution)/shard_map/ar_step/pallas_call | solution.py:415
  97.8 1.3 %copy.10 = f32[2,4,512]{2,1,0:T(4,128)} copy(f32[2,4,512]{2,1,0:T(4,128)} %ar_step.1) | data formatting | bytes 32768

commit v3 on v2

v3 whole, which is shorter than its diff:
```python
import jax
import jax.numpy as jnp
from jax import lax
from jax.experimental import pallas as pl
from jax.experimental.pallas import tpu as pltpu
from jax.sharding import PartitionSpec as P

HEADS = 16
HD = 128
LAT = 128
D = 2048
ROWS = 256
NB = 32
SR = 144
epsilon = 1e-06
masked = -1e30
MESH = pl.DeviceIdType.MESH
f32, bf16 = jnp.float32, jnp.bfloat16
NN = (((1,), (0,)), ((), ()))
NT = (((1,), (1,)), ((), ()))
TN = (((0,), (0,)), ((), ()))
FAR = sorted(
    ((dx, dy) for dx in range(4) for dy in range(4) if dx or dy),
    key=lambda o: -min(o[0], 4 - o[0]) - min(o[1], 4 - o[1]),
)


def dot(a, b, dims):
    return lax.dot_general(a, b, dims, preferred_element_type=f32)


def split3(v):
    hi = v.astype(bf16).astype(f32)
    mid = (v - hi).astype(bf16).astype(f32)
    return hi, mid, v - hi - mid


def stat_rows(*rows):
    ids = lax.broadcasted_iota(jnp.int32, (16, LAT), 0)
    out = jnp.zeros((16, LAT), f32)
    for i, r in enumerate(rows):
        out = jnp.where(ids == i, jnp.broadcast_to(r, (16, LAT)), out)
    return out.astype(bf16)


def stat3(st, i):
    return st[i : i + 1] + st[i + 1 : i + 2] + st[i + 2 : i + 3]


def kernel(
    q_hbm, e_hbm, k_hbm, v_hbm, pos_ref, gain_ref, wt_hbm, wo_hbm, out_ref,
    qbuf, kb, vb, vts, wt, wob, wot, gain2, ob, r1, r2o, r2, ebuf, xs, xb, xr, xn, ub, rb, fb, fx, uf, fu,
    loc_sem, kv_send, kv_recv, w_send, w_recv, g_sem, q_send, q_recv,
    r1_sem, r2_sem, e_sem, x_send, x_recv, u_send, u_recv, xr_sem, f_send, f_recv,
):
    b = lax.axis_index("blk")
    s = lax.axis_index("segment")
    h = b // 2
    zl = b % 2
    zh = s // 2
    c = s % 2
    sib = (b, s + 1 - 2 * c)
    zpart = (b + 1 - 2 * zl, s)

    def rcopy(src, dst, ss, rs, dev):
        return pltpu.make_async_remote_copy(
            src_ref=src, dst_ref=dst, send_sem=ss, recv_sem=rs, device_id=dev, device_id_type=MESH
        )

    def bytes_of(ref, sem):
        pltpu.make_async_copy(ref, ref, sem).wait()

    hx, hy = h // 4, lax.rem(h, 4)

    def chip(dx, dy):
        return lax.rem(hx + dx, 4) * 4 + lax.rem(hy + dy, 4)

    far = [chip(*o) for o in FAR]
    near = [h] + far[::-1]

    half = pl.ds(pl.multiple_of(64 * zl, 64), 64)
    loc = [
        pltpu.make_async_copy(k_hbm.at[c], kb.at[0], loc_sem.at[0]),
        pltpu.make_async_copy(v_hbm.at[c], vb.at[0], loc_sem.at[1]),
        pltpu.make_async_copy(q_hbm.at[c], qbuf.at[b], loc_sem.at[2]),
    ]
    for cp in (loc[2], loc[1], loc[0]):
        cp.start()

    barrier = pltpu.get_barrier_semaphore()
    for dz in range(2):
        for ds in range(4):
            if dz + ds:
                pl.semaphore_signal(
                    barrier, inc=1, device_id=(2 * h + (zl + dz) % 2, (s + ds) % 4), device_id_type=MESH
                )

    for p in far:
        pl.semaphore_signal(barrier, inc=1, device_id=(p * 2 + zl, s), device_id_type=MESH)
    pl.semaphore_wait(barrier, HEADS + 6)

    other = b + 1 - 2 * zl
    q1 = rcopy(q_hbm.at[c], qbuf.at[b], q_send.at[0], q_recv.at[0], zpart)
    q1.start()
    w_to = [
        (wt_hbm, wt.at[c, :, half, :], w_send.at[0], w_recv.at[2 * c + zl]),
        (wo_hbm, wob.at[c, half, :], w_send.at[1], w_recv.at[4 + 2 * c + zl]),
    ]
    w_away = [rcopy(*w, (other, 2 * zh + 1)) for w in w_to]

    @pl.when(c == 0)
    def _():
        for cp in w_away:
            cp.start()

    for p in far:
        rcopy(q_hbm.at[c], qbuf.at[b], q_send.at[0], q_recv.at[1], (p * 2 + zl, s)).start()
    kx = rcopy(k_hbm.at[1 - c], kb.at[1], kv_send.at[0], kv_recv.at[0], sib)
    vx = rcopy(v_hbm.at[1 - c], vb.at[1], kv_send.at[1], kv_recv.at[1], sib)
    gx = rcopy(gain_ref, gain2, g_sem.at[0], g_sem.at[1], sib)
    kx.start()
    vx.start()
    gx.start()
    w_sib = [rcopy(src, dst, w_send.at[2 + i], rs, sib) for i, (src, dst, _, rs) in enumerate(w_to)]
    w_here = [pltpu.make_async_copy(src, dst, rs) for src, dst, _, rs in w_to]

    @pl.when(c == 0)
    def _():
        for cp in w_sib:
            cp.start()

    @pl.when(c == 1)
    def _():
        for cp in w_here:
            cp.start()

    q1.wait_recv()
    for p in far:
        rcopy(qbuf.at[other], qbuf.at[other], q_send.at[0], q_recv.at[1], (p * 2 + zl, s)).start()

    loc[1].wait()
    for j in range(HEADS):
        vts[j, :, 0:ROWS] = vb[0, :, j * HD : (j + 1) * HD].T
    vx.wait_recv()
    for j in range(HEADS):
        vts[j, :, ROWS : 2 * ROWS] = vb[1, :, j * HD : (j + 1) * HD].T
    loc[0].wait()
    kx.wait_recv()
    loc[2].wait()
    bytes_of(qbuf.at[0:30], q_recv.at[1])

    def e_copy(m, t):
        p = lax.rem(h + t, HEADS)
        dst = p * 2 + 1 - m
        cols = pl.ds(pl.multiple_of(p * HD, HD), HD)
        return (
            e_hbm.at[m, :, cols],
            ebuf.at[b],
            dst,
        )

    @pl.when(s == 1)
    def _():
        for m in range(2):
            def e_start(t, _):
                src, dst_ref, dst = e_copy(m, t)
                rcopy(src, dst_ref, e_sem.at[0], e_sem.at[1], (dst, s)).start()
                return 0
            lax.fori_loop(1, HEADS, e_start, 0)
            src, dst_ref, dst = e_copy(m, 0)

            @pl.when(zl == 1 - m)
            def _():
                pltpu.make_async_copy(src, dst_ref, e_sem.at[1]).start()

            @pl.when(zl == m)
            def _():
                rcopy(src, dst_ref, e_sem.at[0], e_sem.at[1], (dst, s)).start()

    base0 = (b * 4 + s) * ROWS
    base1 = (b * 4 + s + 1 - 2 * c) * ROWS
    pos = pos_ref[pl.ds(c, 1), :]
    ids = lax.broadcasted_iota(jnp.int32, (ROWS, LAT), 0)
    scale = HD ** (-0.5)

    ids1 = ids + base1
    ids0 = ids + base0

    def scores(hh):
        cols = pl.ds(pl.multiple_of(hh * HD, HD), HD)
        qh = qbuf[:, :, cols].astype(f32).reshape(LAT, HD).astype(bf16)
        s0 = jnp.where(ids0 < pos, dot(kb[0, :, cols], qh, NT) * scale, masked)
        s1 = jnp.where(ids1 < pos, dot(kb[1, :, cols], qh, NT) * scale, masked)
        return s0, s1

    def weigh(s0, s1):
        top = jnp.maximum(jnp.max(jnp.maximum(s0, s1), axis=0, keepdims=True), 0.1 * masked)
        e0, e1 = jnp.exp(s0 - top), jnp.exp(s1 - top)
        total = jnp.sum(e0 + e1, axis=0, keepdims=True)
        return top, total, jnp.concatenate([e0.astype(bf16), e1.astype(bf16)], axis=0)

    order = far + [h]
    for g in range(0, HEADS, 2):
        group = order[g : g + 2]
        ss = [scores(hh) for hh in group]
        ws = [weigh(*v) for v in ss]
        for hh, (top, total, e) in zip(group, ws):
            ob[hh, 0:HD, :] = dot(vts[hh], e, NN).astype(bf16)
            ob[hh, HD:SR, :] = stat_rows(*split3(top), *split3(total))
        for i in range(g, g + 2):
            if i < HEADS - 1:
                hh = order[i]
                rcopy(ob.at[hh], r1.at[h], r1_sem.at[0], r1_sem.at[1], (hh * 2 + zl, s)).start()

    bytes_of(r1.at[0:15], r1_sem.at[1])
    r1[h] = ob[h]

    def combine(buf, n):
        st = [buf[i, HD:SR, :].astype(f32) for i in range(n)]
        tops = [stat3(v, 0) for v in st]
        top = tops[0]
        for v in tops[1:]:
            top = jnp.maximum(top, v)
        total = jnp.zeros((1, LAT), f32)
        acc = jnp.zeros((HD, LAT), f32)
        for i in range(n):
            w = jnp.exp(tops[i] - top)
            total = total + w * stat3(st[i], 3)
            acc = acc + w * buf[i, 0:HD, :].astype(f32)
        return acc, top, total

    acc, top, total = combine(r1, HEADS)
    r2o[0:HD, :] = acc.astype(bf16)
    r2o[HD:SR, :] = stat_rows(*split3(top), *split3(total))
    z = zh * 2 + zl
    r2_home = (s == 1) & (zl == 1 - c)
    r2_dst = (2 * h + 1 - c, 1)
    r2_copy = rcopy(r2o, r2.at[z], r2_sem.at[0], r2_sem.at[1], r2_dst)

    @pl.when(r2_home)
    def _():
        pltpu.make_async_copy(r2o, r2.at[z], r2_sem.at[1]).start()

    @pl.when(jnp.logical_not(r2_home))
    def _():
        r2_copy.start()

    @pl.when(c == 1)
    def _():
        for cp in w_away:
            cp.start()

    gx.wait_recv()
    my_cols = pl.ds(pl.multiple_of(h * HD, HD), HD)

    def column(ref):
        return jnp.broadcast_to(ref[:, my_cols], (HD, LAT)).T

    seg = h // 4
    jj = lax.broadcasted_iota(jnp.int32, (LAT, LAT), 0)
    ii = lax.broadcasted_iota(jnp.int32, (LAT, LAT), 1)

    def layer(k):
        for p in far:
            rcopy(xs.at[k], xb.at[k, h], x_send.at[k], x_recv.at[k, h], (p * 2 + zl, s)).start()
        pltpu.make_async_copy(xs.at[k], xb.at[k, h], x_recv.at[k, h]).start()
        for i in range(2):
            pltpu.make_async_copy(wt_hbm, wt.at[k, :, 0:64, :], w_recv.at[2 * k + i]).wait()
            pltpu.make_async_copy(wo_hbm, wob.at[k, 0:64, :], w_recv.at[4 + 2 * k + i]).wait()
        for j in range(HEADS):
            wot[k, j] = wob[k, :, j * HD : (j + 1) * HD].T
        if k == 1:

            @pl.when(s == 3)
            def _():
                fb[...] = xn[...].T.reshape(NB, 4, HD)
                sem = f_recv.at[0]
                dst = fx.at[zl, lax.rem(h, 4)]
                for p in far:
                    for dz in range(2):
                        rcopy(fb.at[2 * p + dz], dst, f_send.at[0], sem, (2 * p + dz, seg)).start()
                rcopy(fb.at[other], dst, f_send.at[0], sem, (other, seg)).start()

                @pl.when(seg != s)
                def _():
                    rcopy(fb.at[b], dst, f_send.at[0], sem, (b, seg)).start()

                @pl.when(seg == s)
                def _():
                    pltpu.make_async_copy(fb.at[b], dst, sem).start()

        qkv = jnp.zeros((3 * HD, LAT), f32)
        ss = jnp.zeros((1, LAT), f32)
        for j in range(0, HEADS, 2):
            pair = near[j : j + 2]
            for p in pair:
                pltpu.make_async_copy(xs.at[k], xb.at[k, p], x_recv.at[k, p]).wait()
            w2 = [wt[k, :, :, pl.ds(pl.multiple_of(p * HD, HD), HD)].reshape(3 * HD, HD) for p in pair]
            x2 = [xb[k, p, 0:HD, :] for p in pair]
            qkv = qkv + dot(jnp.concatenate(w2, axis=1), jnp.concatenate(x2, axis=0), NN)
            for p in pair:
                ss = ss + stat3(xb[k, p, HD:SR, :].astype(f32), 0)
        factor = lax.rsqrt(ss * (1.0 / D) + epsilon)
        qkv = (qkv * factor).astype(bf16)
        qt, kt, vt = qkv[0:HD], qkv[HD : 2 * HD], qkv[2 * HD :]
        sc = dot(kt, qt, TN) * scale
        sc = jnp.where(jj <= ii, sc, masked)
        e = jnp.exp(sc - jnp.max(sc, axis=0, keepdims=True))
        soft = (e / jnp.sum(e, axis=0, keepdims=True)).astype(bf16)
        return dot(vt, soft, NN).astype(bf16)

    def exchange(k, att, x0):
        for g in range(0, HEADS - 1, 5):
            us = [dot(wot[k, p], att, NN).astype(bf16) for p in far[g : g + 5]]
            for p, u in zip(far[g : g + 5], us):
                ub[k, p] = u
            for p in far[g : g + 5]:
                rcopy(ub.at[k, p], rb.at[k, h], u_send.at[k], u_recv.at[k], (p * 2 + zl, s)).start()
        x = x0 + dot(wot[k, h], att, NN)
        bytes_of(rb.at[k, 0:15], u_recv.at[k])
        for p in near[1:]:
            x = x + rb[k, p].astype(f32)
        return x

    def pack_x(k, x, gain):
        xs[k, 0:HD, :] = (x * gain).astype(bf16)
        xs[k, HD:SR, :] = stat_rows(*split3(jnp.sum(x * x, axis=0, keepdims=True)))

    @pl.when(c == 1)
    def _():
        @pl.when(s == 1)
        def _():
            bytes_of(ebuf, e_sem.at[1])
            emb = ebuf[...].astype(f32).reshape(LAT, HD).T
            bytes_of(r2, r2_sem.at[1])
            acc, top, total = combine(r2, 4)
            xr[...] = emb + acc / total

        @pl.when(s == 3)
        def _():
            pltpu.make_async_copy(xn, xr, xr_sem.at[1]).wait()

        pack_x(0, xr[...], column(gain2))
        x = exchange(0, layer(0), xr[...])
        xn[...] = x
        pack_x(1, x, column(gain_ref))
        att = layer(1)

        @pl.when(s == 1)
        def _():
            x = exchange(1, att, xn[...])
            fb2 = xr
            fb2[...] = x
            up = rcopy(fb2, xr, xr_sem.at[0], xr_sem.at[1], (other, 3))
            up.start()
            bytes_of(ub.at[1, 0:15], u_send.at[1])
            up.wait_send()

        @pl.when(s == 3)
        def _():
            att_r = att.T
            for n in range(4):
                u = dot(att_r, wob[1, :, n * 512 : (n + 1) * 512], NN)
                uf[n * NB : (n + 1) * NB] = u.reshape(NB, 4, 512).astype(bf16)
            sem = f_recv.at[1]
            dst = fu.at[zl, h]
            for p in far:
                for dz in range(2):
                    for n in range(4):
                        i = 2 * p + dz
                        rcopy(uf.at[n * NB + i], dst, f_send.at[1], sem, (i, n)).start()
            for n in range(4):
                rcopy(uf.at[n * NB + other], dst, f_send.at[1], sem, (other, n)).start()
            for n in range(3):
                rcopy(uf.at[n * NB + b], dst, f_send.at[1], sem, (b, n)).start()
            pltpu.make_async_copy(uf.at[3 * NB + b], dst, sem).start()
            bytes_of(uf.at[0:127], f_send.at[1])

            @pl.when(seg == s)
            def _():
                bytes_of(fb.at[0:31], f_send.at[0])

            @pl.when(seg != s)
            def _():
                bytes_of(fb, f_send.at[0])

        bytes_of(ub.at[0, 0:15], u_send.at[0])
        for k in range(2):
            bytes_of(xb.at[k, 0:15], x_send.at[k])

    bytes_of(qbuf.at[0:31], q_send.at[0])
    bytes_of(ob.at[0:15], r1_sem.at[0])
    for cp in [kx, vx, gx] + w_away:
        cp.wait_send()

    @pl.when(c == 0)
    def _():
        for cp in w_sib:
            cp.wait_send()

    @pl.when(jnp.logical_not(r2_home))
    def _():
        r2_copy.wait_send()

    @pl.when(s == 1)
    def _():
        bytes_of(ebuf.at[0:31], e_sem.at[0])

    bytes_of(fx, f_recv.at[0])
    bytes_of(fu, f_recv.at[1])
    for m in range(2):
        acc = jnp.concatenate([fx[m, i] for i in range(4)], axis=1)
        for i in range(HEADS):
            acc = acc + fu[m, i].astype(f32)
        out_ref[m] = acc


def on_device(
    latent_queries, latent_embed, history_keys, history_values, latent_pos, norm_gain, w_qkv, w_out
):
    wt = jnp.transpose(w_qkv[0], (1, 2, 0))
    hbm = pl.BlockSpec(memory_space=pl.ANY)
    vmem = pl.BlockSpec(memory_space=pltpu.VMEM)
    dma = pltpu.SemaphoreType.DMA
    return pl.pallas_call(
        kernel,
        out_shape=jax.ShapeDtypeStruct((2, 4, 512), f32),
        in_specs=[hbm, hbm, hbm, hbm, vmem, vmem, hbm, hbm],
        out_specs=vmem,
        scratch_shapes=[
            pltpu.VMEM((NB, 4, D), bf16),
            pltpu.VMEM((2, ROWS, D), bf16),
            pltpu.VMEM((2, ROWS, D), bf16),
            pltpu.VMEM((HEADS, HD, 2 * ROWS), bf16),
            pltpu.VMEM((2, 3, HD, D), bf16),
            pltpu.VMEM((2, HD, D), bf16),
            pltpu.VMEM((2, HEADS, HD, HD), bf16),
            pltpu.VMEM((1, D), f32),
            pltpu.VMEM((HEADS, SR, LAT), bf16),
            pltpu.VMEM((HEADS, SR, LAT), bf16),
            pltpu.VMEM((SR, LAT), bf16),
            pltpu.VMEM((4, SR, LAT), bf16),
            pltpu.VMEM((NB, 4, HD), bf16),
            pltpu.VMEM((2, SR, LAT), bf16),
            pltpu.VMEM((2, HEADS, SR, LAT), bf16),
            pltpu.VMEM((HD, LAT), f32),
            pltpu.VMEM((HD, LAT), f32),
            pltpu.VMEM((2, HEADS, HD, LAT), bf16),
            pltpu.VMEM((2, HEADS, HD, LAT), bf16),
            pltpu.VMEM((NB, 4, HD), f32),
            pltpu.VMEM((2, 4, 4, HD), f32),
            pltpu.VMEM((4 * NB, 4, 512), bf16),
            pltpu.VMEM((2, HEADS, 4, 512), bf16),
            dma((3,)), dma((2,)), dma((2,)), dma((4,)), dma((8,)), dma((2,)), dma((1,)), dma((2,)),
            dma((2,)), dma((2,)), dma((2,)), dma((2,)), dma((2, HEADS)), dma((2,)), dma((2,)), dma((2,)), dma((2,)), dma((2,)),
        ],
        compiler_params=pltpu.CompilerParams(
            collective_id=0, has_side_effects=True, vmem_limit_bytes=67043328
        ),
        name="ar_step",
    )(latent_queries, latent_embed, history_keys, history_values, latent_pos, norm_gain, wt, w_out[0])


def solution(mesh):
    return jax.shard_map(
        on_device,
        mesh=mesh,
        in_specs=(
            P(None, "blk", None),
            P(None, "blk", None),
            P(None, ("blk", "segment"), None),
            P(None, ("blk", "segment"), None),
            P(),
            P("segment", None),
            P("segment", None, None, "blk"),
            P("segment", "blk", None),
        ),
        out_specs=P(None, "blk", "segment"),
        check_vma=False,
    )
```

time: 99.4 us -> 89.1 us (0.90)
  Pallas kernels: 97.8 us -> 87.5 us
    pallas_call x1, Pallas kernels: 97.8 us -> 87.5 us  [on_device(): pl.pallas_call(kernel, out_shape=jax.ShapeDtypeStruct((2, 4, 512), f32),...]
where the time goes in v3:
time: 89.1 us; the launch traced here: 88.8 us
  Pallas kernels  87.5 us (98%)
  local copies, waits for them, and re-layouts  1.32 us (1%)
    pallas_call x1, Pallas kernels, on_device(): pl.pallas_call(kernel, out_shape=jax.ShapeDtypeStruct((2, 4, 512), f32),...  87.5 us

profile of v3, /device:TPU:1, one launch (start us, length us, event | category | flops | bytes accessed | tf_op | source)
XLA Modules:
  0.0 88.8 jit_solution(4812431941146665813)
XLA Ops:
  0.0 87.5 %ar_step.1 = f32[2,4,512]{2,1,0:T(4,128)} custom-call(bf16[2,4,2048]{2,1,0:T(4,128)(2,1)} %q_hbm.1, bf16[2,4,2048]{2,1,0:T(4,128)(2,1)} %e_hbm.1, bf16[2,256,2048]{2,1,0:T(8,128)(2,1)} %k_hbm.1, bf16[2,256,2048]{2,1,0:T(8,128)(2,1)} %v_hbm.1, s32[2,128]{1,0:T(2,128)} %pos_ref.1, f32[1,2048]{1,0:T(1,128)} %gain_ref.1, bf16[3,64,2048]{2,1,0:T(8,128)(2,1)} %bitcast.4, ...), custom_call_target="tpu_custom_call" | custom-call | tf_op jit(solution)/shard_map/ar_step/pallas_call | solution.py:425
  87.5 1.3 %copy.10 = f32[2,4,512]{2,1,0:T(4,128)} copy(f32[2,4,512]{2,1,0:T(4,128)} %ar_step.1) | data formatting | bytes 32768

commit v4 on v3

--- a/solution.py
+++ b/solution.py
@@ -19,10 +19,21 @@
 NN = (((1,), (0,)), ((), ()))
 NT = (((1,), (1,)), ((), ()))
 TN = (((0,), (0,)), ((), ()))
-FAR = sorted(
-    ((dx, dy) for dx in range(4) for dy in range(4) if dx or dy),
-    key=lambda o: -min(o[0], 4 - o[0]) - min(o[1], 4 - o[1]),
+
+
+def hops(o):
+    return sum(min(v, 4 - v) for v in o)
+
+
+FAR = sorted(((dx, dy) for dx in range(4) for dy in range(4) if dx or dy), key=lambda o: -hops(o))
+FAR3 = sorted(
+    ((dx, dy, dz) for dx in range(4) for dy in range(4) for dz in range(2) if dx or dy or dz),
+    key=lambda o: -hops(o),
 )
+HALVES = [
+    sorted(((dx, dy) for dx in steps for dy in range(4)), key=lambda o: -hops(o)) for steps in ((2, 1), (3, 0))
+]
+NEAR = 10
 
 
 def dot(a, b, dims):
@@ -48,8 +59,8 @@
 
 
 def kernel(
-    q_hbm, e_hbm, k_hbm, v_hbm, pos_ref, gain_ref, wt_hbm, wo_hbm, out_ref,
-    qbuf, kb, vb, vts, wt, wob, wot, gain2, ob, r1, r2o, r2, ebuf, xs, xb, xr, xn, ub, rb, fb, fx, uf, fu,
+    q_hbm, e_hbm, k_hbm, v_hbm, pos_hbm, gain_hbm, wt_hbm, wo_hbm, out_ref,
+    pos_ref, gain_ref, qbuf, kb, vb, vts, wt, wob, wot, gain2, gain3, ob, r1, r2o, r2, ebuf, xs, xb, xr, xn, ub, rb, fb, fx, uf, fu,
     loc_sem, kv_send, kv_recv, w_send, w_recv, g_sem, q_send, q_recv,
     r1_sem, r2_sem, e_sem, x_send, x_recv, u_send, u_recv, xr_sem, f_send, f_recv,
 ):
@@ -83,25 +94,41 @@
         pltpu.make_async_copy(k_hbm.at[c], kb.at[0], loc_sem.at[0]),
         pltpu.make_async_copy(v_hbm.at[c], vb.at[0], loc_sem.at[1]),
         pltpu.make_async_copy(q_hbm.at[c], qbuf.at[b], loc_sem.at[2]),
+        pltpu.make_async_copy(pos_hbm, pos_ref, loc_sem.at[3]),
+        pltpu.make_async_copy(gain_hbm, gain_ref, loc_sem.at[4]),
     ]
-    for cp in (loc[2], loc[1], loc[0]):
+    barrier = pltpu.get_barrier_semaphore()
+    other = b + 1 - 2 * zl
+
+    def pair_dev(dx, dy, dz):
+        return chip(dx, dy) * 2 + (1 - zl if dz else zl)
+
+    for o in FAR3:
+        pl.semaphore_signal(barrier, inc=1, device_id=(pair_dev(*o), s), device_id_type=MESH)
+    for blk in (b, other):
+        for ds in range(1, 4):
+            pl.semaphore_signal(barrier, inc=1, device_id=(blk, (s + ds) % 4), device_id_type=MESH)
+    for cp in (loc[2], loc[1], loc[0], loc[3], loc[4]):
         cp.start()
 
-    barrier = pltpu.get_barrier_semaphore()
-    for dz in range(2):
-        for ds in range(4):
-            if dz + ds:
-                pl.semaphore_signal(
-                    barrier, inc=1, device_id=(2 * h + (zl + dz) % 2, (s + ds) % 4), device_id_type=MESH
-                )
-
-    for p in far:
-        pl.semaphore_signal(barrier, inc=1, device_id=(p * 2 + zl, s), device_id_type=MESH)
-    pl.semaphore_wait(barrier, HEADS + 6)
-
-    other = b + 1 - 2 * zl
-    q1 = rcopy(q_hbm.at[c], qbuf.at[b], q_send.at[0], q_recv.at[0], zpart)
-    q1.start()
+    pl.semaphore_wait(barrier, 37)
+
+    kx = rcopy(k_hbm.at[1 - c], kb.at[1], kv_send.at[0], kv_recv.at[0], sib)
+    vx = rcopy(v_hbm.at[1 - c], vb.at[1], kv_send.at[1], kv_recv.at[1], sib)
+    kx.start()
+    vx.start()
+
+    def q_start(half_no):
+        for dx, dy, dz in FAR3:
+            for step in ((2, 1), (3, 0))[half_no]:
+                cols = pl.ds(pl.multiple_of(lax.rem(hx + dx + step, 4) * 512, 512), 512)
+                rcopy(
+                    q_hbm.at[c, :, cols], qbuf.at[b, :, cols], q_send.at[0], q_recv.at[half_no],
+                    (pair_dev(dx, dy, dz), s),
+                ).start()
+
+    q_start(0)
+    q_start(1)
     w_to = [
         (wt_hbm, wt.at[c, :, half, :], w_send.at[0], w_recv.at[2 * c + zl]),
         (wo_hbm, wob.at[c, half, :], w_send.at[1], w_recv.at[4 + 2 * c + zl]),
@@ -110,17 +137,16 @@
 
     @pl.when(c == 0)
     def _():
-        for cp in w_away:
-            cp.start()
-
-    for p in far:
-        rcopy(q_hbm.at[c], qbuf.at[b], q_send.at[0], q_recv.at[1], (p * 2 + zl, s)).start()
-    kx = rcopy(k_hbm.at[1 - c], kb.at[1], kv_send.at[0], kv_recv.at[0], sib)
-    vx = rcopy(v_hbm.at[1 - c], vb.at[1], kv_send.at[1], kv_recv.at[1], sib)
-    gx = rcopy(gain_ref, gain2, g_sem.at[0], g_sem.at[1], sib)
-    kx.start()
-    vx.start()
+        w_away[0].start()
+
+    gx = rcopy(gain_hbm, gain2, g_sem.at[0], g_sem.at[1], sib)
     gx.start()
+    g3 = rcopy(gain_hbm, gain3, g_sem.at[2], g_sem.at[3], (other, 1))
+
+    @pl.when(s == 2)
+    def _():
+        g3.start()
+
     w_sib = [rcopy(src, dst, w_send.at[2 + i], rs, sib) for i, (src, dst, _, rs) in enumerate(w_to)]
     w_here = [pltpu.make_async_copy(src, dst, rs) for src, dst, _, rs in w_to]
 
@@ -134,20 +160,14 @@
         for cp in w_here:
             cp.start()
 
-    q1.wait_recv()
-    for p in far:
-        rcopy(qbuf.at[other], qbuf.at[other], q_send.at[0], q_recv.at[1], (p * 2 + zl, s)).start()
-
     loc[1].wait()
     for j in range(HEADS):
-        vts[j, :, 0:ROWS] = vb[0, :, j * HD : (j + 1) * HD].T
-    vx.wait_recv()
-    for j in range(HEADS):
-        vts[j, :, ROWS : 2 * ROWS] = vb[1, :, j * HD : (j + 1) * HD].T
+        vts[j] = vb[0, :, j * HD : (j + 1) * HD].T
     loc[0].wait()
     kx.wait_recv()
-    loc[2].wait()
-    bytes_of(qbuf.at[0:30], q_recv.at[1])
+    for cp in loc[2:]:
+        cp.wait()
+    bytes_of(qbuf.at[0:31, :, 0:1024], q_recv.at[0])
 
     def e_copy(m, t):
         p = lax.rem(h + t, HEADS)
@@ -197,15 +217,20 @@
         top = jnp.maximum(jnp.max(jnp.maximum(s0, s1), axis=0, keepdims=True), 0.1 * masked)
         e0, e1 = jnp.exp(s0 - top), jnp.exp(s1 - top)
         total = jnp.sum(e0 + e1, axis=0, keepdims=True)
-        return top, total, jnp.concatenate([e0.astype(bf16), e1.astype(bf16)], axis=0)
-
-    order = far + [h]
+        return top, total, e0.astype(bf16), e1.astype(bf16)
+
+    order = [chip(*o) for o in HALVES[0] + HALVES[1]]
     for g in range(0, HEADS, 2):
+        if g == HEADS // 2:
+            bytes_of(qbuf.at[0:31, :, 0:1024], q_recv.at[1])
         group = order[g : g + 2]
         ss = [scores(hh) for hh in group]
         ws = [weigh(*v) for v in ss]
-        for hh, (top, total, e) in zip(group, ws):
-            ob[hh, 0:HD, :] = dot(vts[hh], e, NN).astype(bf16)
+        if g == 0:
+            vx.wait_recv()
+        for hh, (top, total, e0, e1) in zip(group, ws):
+            cols = pl.ds(pl.multiple_of(hh * HD, HD), HD)
+            ob[hh, 0:HD, :] = (dot(vts[hh], e0, NN) + dot(vb[1, :, cols].T, e1, NN)).astype(bf16)
             ob[hh, HD:SR, :] = stat_rows(*split3(top), *split3(total))
         for i in range(g, g + 2):
             if i < HEADS - 1:
@@ -247,8 +272,9 @@
 
     @pl.when(c == 1)
     def _():
-        for cp in w_away:
-            cp.start()
+        w_away[0].start()
+
+    w_away[1].start()
 
     gx.wait_recv()
     my_cols = pl.ds(pl.multiple_of(h * HD, HD), HD)
@@ -260,15 +286,27 @@
     jj = lax.broadcasted_iota(jnp.int32, (LAT, LAT), 0)
     ii = lax.broadcasted_iota(jnp.int32, (LAT, LAT), 1)
 
-    def layer(k):
-        for p in far:
-            rcopy(xs.at[k], xb.at[k, h], x_send.at[k], x_recv.at[k, h], (p * 2 + zl, s)).start()
-        pltpu.make_async_copy(xs.at[k], xb.at[k, h], x_recv.at[k, h]).start()
+    halves = (slice(0, 64), slice(64, SR))
+
+    def pack_x(k, i, x, gain, before):
+        xs[k, 64 * i : 64 * i + 64, :] = (x * gain[64 * i : 64 * i + 64]).astype(bf16)
+        ss = before + jnp.sum(x * x, axis=0, keepdims=True)
+        if i:
+            xs[k, HD:SR, :] = stat_rows(*split3(ss))
+        return ss
+
+    def gather(k, i):
+        rows = halves[i]
+        for n, p in enumerate(far):
+            late = 1 if n < HEADS - NEAR else 0
+            rcopy(
+                xs.at[k, rows], xb.at[k, h, rows], x_send.at[k], x_recv.at[k, late], (p * 2 + zl, s)
+            ).start()
+        pltpu.make_async_copy(xs.at[k, rows], xb.at[k, h, rows], x_recv.at[k, 0]).start()
+
+    def attend(k):
         for i in range(2):
             pltpu.make_async_copy(wt_hbm, wt.at[k, :, 0:64, :], w_recv.at[2 * k + i]).wait()
-            pltpu.make_async_copy(wo_hbm, wob.at[k, 0:64, :], w_recv.at[4 + 2 * k + i]).wait()
-        for j in range(HEADS):
-            wot[k, j] = wob[k, :, j * HD : (j + 1) * HD].T
         if k == 1:
 
             @pl.when(s == 3)
@@ -293,8 +331,14 @@
         ss = jnp.zeros((1, LAT), f32)
         for j in range(0, HEADS, 2):
             pair = near[j : j + 2]
-            for p in pair:
-                pltpu.make_async_copy(xs.at[k], xb.at[k, p], x_recv.at[k, p]).wait()
+            if j == 0:
+                bytes_of(xb.at[k, 0:NEAR], x_recv.at[k, 0])
+            if j == NEAR:
+                for i in range(2):
+                    pltpu.make_async_copy(wo_hbm, wob.at[k, 0:64, :], w_recv.at[4 + 2 * k + i]).wait()
+                for i in range(HEADS):
+                    wot[k, i] = wob[k, :, i * HD : (i + 1) * HD].T
+                bytes_of(xb.at[k, 0 : HEADS - NEAR], x_recv.at[k, 1])
             w2 = [wt[k, :, :, pl.ds(pl.multiple_of(p * HD, HD), HD)].reshape(3 * HD, HD) for p in pair]
             x2 = [xb[k, p, 0:HD, :] for p in pair]
             qkv = qkv + dot(jnp.concatenate(w2, axis=1), jnp.concatenate(x2, axis=0), NN)
@@ -309,22 +353,26 @@
         soft = (e / jnp.sum(e, axis=0, keepdims=True)).astype(bf16)
         return dot(vt, soft, NN).astype(bf16)
 
-    def exchange(k, att, x0):
-        for g in range(0, HEADS - 1, 5):
-            us = [dot(wot[k, p], att, NN).astype(bf16) for p in far[g : g + 5]]
-            for p, u in zip(far[g : g + 5], us):
-                ub[k, p] = u
-            for p in far[g : g + 5]:
-                rcopy(ub.at[k, p], rb.at[k, h], u_send.at[k], u_recv.at[k], (p * 2 + zl, s)).start()
-        x = x0 + dot(wot[k, h], att, NN)
-        bytes_of(rb.at[k, 0:15], u_recv.at[k])
-        for p in near[1:]:
-            x = x + rb[k, p].astype(f32)
-        return x
-
-    def pack_x(k, x, gain):
-        xs[k, 0:HD, :] = (x * gain).astype(bf16)
-        xs[k, HD:SR, :] = stat_rows(*split3(jnp.sum(x * x, axis=0, keepdims=True)))
+    def exchange(k, att, x_ref, done):
+        for i in range(2):
+            rows = slice(64 * i, 64 * i + 64)
+            for g in range(0, HEADS - 1, 5):
+                us = [dot(wot[k, p, rows, :], att, NN).astype(bf16) for p in far[g : g + 5]]
+                for p, u in zip(far[g : g + 5], us):
+                    ub[k, p, rows, :] = u
+                for p in far[g : g + 5]:
+                    rcopy(
+                        ub.at[k, p, rows], rb.at[k, h, rows], u_send.at[k], u_recv.at[k, i], (p * 2 + zl, s)
+                    ).start()
+        own = dot(wot[k, h], att, NN)
+        ss = jnp.zeros((1, LAT), f32)
+        for i in range(2):
+            rows = slice(64 * i, 64 * i + 64)
+            x = x_ref[rows, :] + own[rows]
+            bytes_of(rb.at[k, 0:15, rows], u_recv.at[k, i])
+            for p in near[1:]:
+                x = x + rb[k, p, rows, :].astype(f32)
+            ss = done(i, x, ss)
 
     @pl.when(c == 1)
     def _():
@@ -335,24 +383,50 @@
             bytes_of(r2, r2_sem.at[1])
             acc, top, total = combine(r2, 4)
             xr[...] = emb + acc / total
+            ss = jnp.zeros((1, LAT), f32)
+            for i in range(2):
+                ss = pack_x(0, i, xr[64 * i : 64 * i + 64, :], column(gain2), ss)
+                gather(0, i)
 
         @pl.when(s == 3)
         def _():
-            pltpu.make_async_copy(xn, xr, xr_sem.at[1]).wait()
-
-        pack_x(0, xr[...], column(gain2))
-        x = exchange(0, layer(0), xr[...])
-        xn[...] = x
-        pack_x(1, x, column(gain_ref))
-        att = layer(1)
+            for i in range(2):
+                bytes_of(xs.at[0, halves[i]], xr_sem.at[3 + i])
+                gather(0, i)
+
+        att = attend(0)
+
+        @pl.when(s == 3)
+        def _():
+            bytes_of(xr, xr_sem.at[1])
+
+        def to_next(i, x, ss):
+            xn[64 * i : 64 * i + 64, :] = x
+            ss = pack_x(1, i, x, column(gain_ref), ss)
+            gather(1, i)
+            return ss
+
+        exchange(0, att, xr, to_next)
+        att = attend(1)
 
         @pl.when(s == 1)
         def _():
-            x = exchange(1, att, xn[...])
-            fb2 = xr
-            fb2[...] = x
-            up = rcopy(fb2, xr, xr_sem.at[0], xr_sem.at[1], (other, 3))
+            bytes_of(gain3, g_sem.at[3])
+
+            def over(i):
+                rows = halves[i]
+                return rcopy(xs.at[2, rows], xs.at[0, rows], xr_sem.at[2], xr_sem.at[3 + i], (other, 3))
+
+            def to_plane(i, x, ss):
+                xr[64 * i : 64 * i + 64, :] = x
+                ss = pack_x(2, i, x, column(gain3), ss)
+                over(i).start()
+                return ss
+
+            exchange(1, att, xn, to_plane)
+            up = rcopy(xr, xr, xr_sem.at[0], xr_sem.at[1], (other, 3))
             up.start()
+            bytes_of(xs.at[2], xr_sem.at[2])
             bytes_of(ub.at[1, 0:15], u_send.at[1])
             up.wait_send()
 
@@ -398,6 +472,10 @@
         for cp in w_sib:
             cp.wait_send()
 
+    @pl.when(s == 2)
+    def _():
+        g3.wait_send()
+
     @pl.when(jnp.logical_not(r2_home))
     def _():
         r2_copy.wait_send()
@@ -425,23 +503,26 @@
     return pl.pallas_call(
         kernel,
         out_shape=jax.ShapeDtypeStruct((2, 4, 512), f32),
-        in_specs=[hbm, hbm, hbm, hbm, vmem, vmem, hbm, hbm],
+        in_specs=[hbm] * 8,
         out_specs=vmem,
         scratch_shapes=[
+            pltpu.VMEM((2, LAT), jnp.int32),
+            pltpu.VMEM((1, D), f32),
             pltpu.VMEM((NB, 4, D), bf16),
             pltpu.VMEM((2, ROWS, D), bf16),
             pltpu.VMEM((2, ROWS, D), bf16),
-            pltpu.VMEM((HEADS, HD, 2 * ROWS), bf16),
+            pltpu.VMEM((HEADS, HD, ROWS), bf16),
             pltpu.VMEM((2, 3, HD, D), bf16),
             pltpu.VMEM((2, HD, D), bf16),
             pltpu.VMEM((2, HEADS, HD, HD), bf16),
+            pltpu.VMEM((1, D), f32),
             pltpu.VMEM((1, D), f32),
             pltpu.VMEM((HEADS, SR, LAT), bf16),
             pltpu.VMEM((HEADS, SR, LAT), bf16),
             pltpu.VMEM((SR, LAT), bf16),
             pltpu.VMEM((4, SR, LAT), bf16),
             pltpu.VMEM((NB, 4, HD), bf16),
-            pltpu.VMEM((2, SR, LAT), bf16),
+            pltpu.VMEM((3, SR, LAT), bf16),
             pltpu.VMEM((2, HEADS, SR, LAT), bf16),
             pltpu.VMEM((HD, LAT), f32),
             pltpu.VMEM((HD, LAT), f32),
@@ -451,8 +532,8 @@
             pltpu.VMEM((2, 4, 4, HD), f32),
             pltpu.VMEM((4 * NB, 4, 512), bf16),
             pltpu.VMEM((2, HEADS, 4, 512), bf16),
-            dma((3,)), dma((2,)), dma((2,)), dma((4,)), dma((8,)), dma((2,)), dma((1,)), dma((2,)),
-            dma((2,)), dma((2,)), dma((2,)), dma((2,)), dma((2, HEADS)), dma((2,)), dma((2,)), dma((2,)), dma((2,)), dma((2,)),
+            dma((5,)), dma((2,)), dma((2,)), dma((4,)), dma((8,)), dma((4,)), dma((1,)), dma((2,)),
+            dma((2,)), dma((2,)), dma((2,)), dma((2,)), dma((2, 2)), dma((2,)), dma((2, 2)), dma((5,)), dma((2,)), dma((2,)),
         ],
         compiler_params=pltpu.CompilerParams(
             collective_id=0, has_side_effects=True, vmem_limit_bytes=67043328

time: 89.1 us -> 84.4 us (0.947)
  Pallas kernels: 87.5 us -> 82.9 us
    pallas_call x1, Pallas kernels: 87.5 us -> 82.9 us  [on_device(): pl.pallas_call(kernel, out_shape=jax.ShapeDtypeStruct((2, 4, 512), f32),...]
where the time goes in v4:
time: 84.4 us; the launch traced here: 84.3 us
  Pallas kernels  82.9 us (98%)
  local copies, waits for them, and re-layouts  1.32 us (2%)
    pallas_call x1, Pallas kernels, on_device(): pl.pallas_call(kernel, out_shape=jax.ShapeDtypeStruct((2, 4, 512), f32),...  82.9 us

profile of v4, /device:TPU:1, one launch (start us, length us, event | category | flops | bytes accessed | tf_op | source)
XLA Modules:
  0.0 84.3 jit_solution(18290225066706287280)
XLA Ops:
  0.0 82.9 %ar_step.1 = f32[2,4,512]{2,1,0:T(4,128)} custom-call(bf16[2,4,2048]{2,1,0:T(4,128)(2,1)} %q_hbm.1, bf16[2,4,2048]{2,1,0:T(4,128)(2,1)} %e_hbm.1, bf16[2,256,2048]{2,1,0:T(8,128)(2,1)} %k_hbm.1, bf16[2,256,2048]{2,1,0:T(8,128)(2,1)} %v_hbm.1, s32[2,128]{1,0:T(2,128)} %pos_hbm.1, f32[1,2048]{1,0:T(1,128)} %gain_hbm.1, bf16[3,64,2048]{2,1,0:T(8,128)(2,1)} %bitcast.4, ...), custom_call_target="tpu_custom_call" | custom-call | tf_op jit(solution)/shard_map/ar_step/pallas_call | solution.py:503
  82.9 1.3 %copy.10 = f32[2,4,512]{2,1,0:T(4,128)} copy(f32[2,4,512]{2,1,0:T(4,128)} %ar_step.1) | data formatting | bytes 32768

commit v5 on v4

--- a/solution.py
+++ b/solution.py
@@ -60,9 +60,9 @@
 
 def kernel(
     q_hbm, e_hbm, k_hbm, v_hbm, pos_hbm, gain_hbm, wt_hbm, wo_hbm, out_ref,
-    pos_ref, gain_ref, qbuf, kb, vb, vts, wt, wob, wot, gain2, gain3, ob, r1, r2o, r2, ebuf, xs, xb, xr, xn, ub, rb, fb, fx, uf, fu,
+    pos_ref, gains, qbuf, kb, vb, vts, wt, wob, wot, ob, r1, r2o, r2, ebuf, xs, xb, xf, ub, rb, fb, fx, uf, fu,
     loc_sem, kv_send, kv_recv, w_send, w_recv, g_sem, q_send, q_recv,
-    r1_sem, r2_sem, e_sem, x_send, x_recv, u_send, u_recv, xr_sem, f_send, f_recv,
+    r1_sem, r2_sem, e_sem, x_send, x_recv, u_send, u_recv, f_send, f_recv, go_sem,
 ):
     b = lax.axis_index("blk")
     s = lax.axis_index("segment")
@@ -95,7 +95,6 @@
         pltpu.make_async_copy(v_hbm.at[c], vb.at[0], loc_sem.at[1]),
         pltpu.make_async_copy(q_hbm.at[c], qbuf.at[b], loc_sem.at[2]),
         pltpu.make_async_copy(pos_hbm, pos_ref, loc_sem.at[3]),
-        pltpu.make_async_copy(gain_hbm, gain_ref, loc_sem.at[4]),
     ]
     barrier = pltpu.get_barrier_semaphore()
     other = b + 1 - 2 * zl
@@ -108,7 +107,7 @@
     for blk in (b, other):
         for ds in range(1, 4):
             pl.semaphore_signal(barrier, inc=1, device_id=(blk, (s + ds) % 4), device_id_type=MESH)
-    for cp in (loc[2], loc[1], loc[0], loc[3], loc[4]):
+    for cp in (loc[2], loc[1], loc[0], loc[3]):
         cp.start()
 
     pl.semaphore_wait(barrier, 37)
@@ -130,34 +129,28 @@
     q_start(0)
     q_start(1)
     w_to = [
-        (wt_hbm, wt.at[c, :, half, :], w_send.at[0], w_recv.at[2 * c + zl]),
-        (wo_hbm, wob.at[c, half, :], w_send.at[1], w_recv.at[4 + 2 * c + zl]),
+        (wt_hbm, wt.at[s, :, half, :], w_recv.at[s]),
+        (wo_hbm, wob.at[s, half, :], w_recv.at[4 + s]),
     ]
-    w_away = [rcopy(*w, (other, 2 * zh + 1)) for w in w_to]
-
-    @pl.when(c == 0)
-    def _():
+    w_away = [rcopy(src, dst, w_send.at[i], rs, (other, 1)) for i, (src, dst, rs) in enumerate(w_to)]
+    w_same = [rcopy(src, dst, w_send.at[2 + i], rs, (b, 1)) for i, (src, dst, rs) in enumerate(w_to)]
+    gx = rcopy(gain_hbm, gains.at[s], g_sem.at[0], g_sem.at[1], (b, 1))
+
+    @pl.when(s == 1)
+    def _():
+        for src, dst, rs in w_to:
+            pltpu.make_async_copy(src, dst, rs).start()
+        pltpu.make_async_copy(gain_hbm, gains.at[s], g_sem.at[1]).start()
+
+    @pl.when(s != 1)
+    def _():
+        gx.start()
         w_away[0].start()
 
-    gx = rcopy(gain_hbm, gain2, g_sem.at[0], g_sem.at[1], sib)
-    gx.start()
-    g3 = rcopy(gain_hbm, gain3, g_sem.at[2], g_sem.at[3], (other, 1))
-
-    @pl.when(s == 2)
-    def _():
-        g3.start()
-
-    w_sib = [rcopy(src, dst, w_send.at[2 + i], rs, sib) for i, (src, dst, _, rs) in enumerate(w_to)]
-    w_here = [pltpu.make_async_copy(src, dst, rs) for src, dst, _, rs in w_to]
-
-    @pl.when(c == 0)
-    def _():
-        for cp in w_sib:
-            cp.start()
-
-    @pl.when(c == 1)
-    def _():
-        for cp in w_here:
+    @pl.when(s == 0)
+    def _():
+        w_away[1].start()
+        for cp in w_same:
             cp.start()
 
     loc[1].wait()
@@ -270,17 +263,16 @@
     def _():
         r2_copy.start()
 
-    @pl.when(c == 1)
-    def _():
-        w_away[0].start()
-
-    w_away[1].start()
-
-    gx.wait_recv()
+    @pl.when(zh == 1)
+    def _():
+        pl.semaphore_wait(go_sem, 2)
+        for cp in [w_away[1]] + w_same:
+            cp.start()
+
     my_cols = pl.ds(pl.multiple_of(h * HD, HD), HD)
 
-    def column(ref):
-        return jnp.broadcast_to(ref[:, my_cols], (HD, LAT)).T
+    def column(k):
+        return jnp.broadcast_to(gains[k, :, my_cols], (HD, LAT)).T
 
     seg = h // 4
     jj = lax.broadcasted_iota(jnp.int32, (LAT, LAT), 0)
@@ -300,32 +292,28 @@
         for n, p in enumerate(far):
             late = 1 if n < HEADS - NEAR else 0
             rcopy(
-                xs.at[k, rows], xb.at[k, h, rows], x_send.at[k], x_recv.at[k, late], (p * 2 + zl, s)
+                xs.at[k, rows], xb.at[k, h, rows], x_send.at[0], x_recv.at[k, late], (p * 2 + zl, s)
             ).start()
         pltpu.make_async_copy(xs.at[k, rows], xb.at[k, h, rows], x_recv.at[k, 0]).start()
 
     def attend(k):
-        for i in range(2):
-            pltpu.make_async_copy(wt_hbm, wt.at[k, :, 0:64, :], w_recv.at[2 * k + i]).wait()
-        if k == 1:
-
-            @pl.when(s == 3)
+        bytes_of(wt.at[k], w_recv.at[k])
+        if k == 3:
+            fb[...] = xf[k].T.reshape(NB, 4, HD)
+            sem = f_recv.at[0]
+            dst = fx.at[1 - zl, lax.rem(h, 4)]
+            for p in far:
+                for dz in range(2):
+                    rcopy(fb.at[2 * p + dz], dst, f_send.at[0], sem, (2 * p + dz, seg)).start()
+            rcopy(fb.at[other], dst, f_send.at[0], sem, (other, seg)).start()
+
+            @pl.when(seg != s)
             def _():
-                fb[...] = xn[...].T.reshape(NB, 4, HD)
-                sem = f_recv.at[0]
-                dst = fx.at[zl, lax.rem(h, 4)]
-                for p in far:
-                    for dz in range(2):
-                        rcopy(fb.at[2 * p + dz], dst, f_send.at[0], sem, (2 * p + dz, seg)).start()
-                rcopy(fb.at[other], dst, f_send.at[0], sem, (other, seg)).start()
-
-                @pl.when(seg != s)
-                def _():
-                    rcopy(fb.at[b], dst, f_send.at[0], sem, (b, seg)).start()
-
-                @pl.when(seg == s)
-                def _():
-                    pltpu.make_async_copy(fb.at[b], dst, sem).start()
+                rcopy(fb.at[b], dst, f_send.at[0], sem, (b, seg)).start()
+
+            @pl.when(seg == s)
+            def _():
+                pltpu.make_async_copy(fb.at[b], dst, sem).start()
 
         qkv = jnp.zeros((3 * HD, LAT), f32)
         ss = jnp.zeros((1, LAT), f32)
@@ -334,9 +322,8 @@
             if j == 0:
                 bytes_of(xb.at[k, 0:NEAR], x_recv.at[k, 0])
             if j == NEAR:
-                for i in range(2):
-                    pltpu.make_async_copy(wo_hbm, wob.at[k, 0:64, :], w_recv.at[4 + 2 * k + i]).wait()
-                for i in range(HEADS):
+                bytes_of(wob.at[k], w_recv.at[4 + k])
+                for i in range(HEADS if k < 3 else 0):
                     wot[k, i] = wob[k, :, i * HD : (i + 1) * HD].T
                 bytes_of(xb.at[k, 0 : HEADS - NEAR], x_recv.at[k, 1])
             w2 = [wt[k, :, :, pl.ds(pl.multiple_of(p * HD, HD), HD)].reshape(3 * HD, HD) for p in pair]
@@ -353,128 +340,96 @@
         soft = (e / jnp.sum(e, axis=0, keepdims=True)).astype(bf16)
         return dot(vt, soft, NN).astype(bf16)
 
-    def exchange(k, att, x_ref, done):
+    def exchange(k, att):
         for i in range(2):
             rows = slice(64 * i, 64 * i + 64)
-            for g in range(0, HEADS - 1, 5):
-                us = [dot(wot[k, p, rows, :], att, NN).astype(bf16) for p in far[g : g + 5]]
-                for p, u in zip(far[g : g + 5], us):
+            for group in (far[0:5], far[5:15]) if i == 0 else (far,):
+                us = [dot(wot[k, p, rows, :], att, NN).astype(bf16) for p in group]
+                for p, u in zip(group, us):
                     ub[k, p, rows, :] = u
-                for p in far[g : g + 5]:
+                for p in group:
                     rcopy(
-                        ub.at[k, p, rows], rb.at[k, h, rows], u_send.at[k], u_recv.at[k, i], (p * 2 + zl, s)
+                        ub.at[k, p, rows], rb.at[k, h, rows], u_send.at[0], u_recv.at[k, i], (p * 2 + zl, s)
                     ).start()
         own = dot(wot[k, h], att, NN)
         ss = jnp.zeros((1, LAT), f32)
         for i in range(2):
             rows = slice(64 * i, 64 * i + 64)
-            x = x_ref[rows, :] + own[rows]
+            x = xf[k, rows, :] + own[rows]
             bytes_of(rb.at[k, 0:15, rows], u_recv.at[k, i])
             for p in near[1:]:
                 x = x + rb[k, p, rows, :].astype(f32)
-            ss = done(i, x, ss)
-
-    @pl.when(c == 1)
-    def _():
-        @pl.when(s == 1)
+            xf[k + 1, rows, :] = x
+            ss = pack_x(k + 1, i, x, column(k + 1), ss)
+            gather(k + 1, i)
+
+    @pl.when(s == 1)
+    def _():
+        bytes_of(gains, g_sem.at[1])
+        bytes_of(ebuf, e_sem.at[1])
+        emb = ebuf[...].astype(f32).reshape(LAT, HD).T
+        bytes_of(r2, r2_sem.at[1])
+        acc, top, total = combine(r2, 4)
+        x0 = emb + acc / total
+        xf[0] = x0
+        ss = jnp.zeros((1, LAT), f32)
+        for i in range(2):
+            ss = pack_x(0, i, x0[64 * i : 64 * i + 64], column(0), ss)
+            gather(0, i)
+
+        def signal(dev):
+            pl.semaphore_signal(go_sem, inc=1, device_id=dev, device_id_type=MESH)
+
+        signal((other, 1))
+        signal((b, 2))
+        signal((other, 2))
+        pl.semaphore_wait(go_sem, 1)
+        for cp in w_away:
+            cp.start()
+        exchange(0, attend(0))
+        signal((b, 3))
+        signal((other, 3))
+        for k in range(1, 3):
+            exchange(k, attend(k))
+        att = attend(3)
+        att_r = att.T
+        sem = f_recv.at[1]
+        dst = fu.at[1 - zl, h]
+        for n in range(4):
+            u = dot(att_r, wob[3, :, n * 512 : (n + 1) * 512], NN)
+            uf[n * NB : (n + 1) * NB] = u.reshape(NB, 4, 512).astype(bf16)
+        for p in far:
+            for dz in range(2):
+                for n in range(4):
+                    i = 2 * p + dz
+                    rcopy(uf.at[n * NB + i], dst, f_send.at[1], sem, (i, n)).start()
+        for n in range(4):
+            rcopy(uf.at[n * NB + other], dst, f_send.at[1], sem, (other, n)).start()
+        for n in (0, 2, 3):
+            rcopy(uf.at[n * NB + b], dst, f_send.at[1], sem, (b, n)).start()
+        pltpu.make_async_copy(uf.at[NB + b], dst, sem).start()
+        bytes_of(uf.at[0:127], f_send.at[1])
+
+        @pl.when(seg == s)
         def _():
-            bytes_of(ebuf, e_sem.at[1])
-            emb = ebuf[...].astype(f32).reshape(LAT, HD).T
-            bytes_of(r2, r2_sem.at[1])
-            acc, top, total = combine(r2, 4)
-            xr[...] = emb + acc / total
-            ss = jnp.zeros((1, LAT), f32)
-            for i in range(2):
-                ss = pack_x(0, i, xr[64 * i : 64 * i + 64, :], column(gain2), ss)
-                gather(0, i)
-
-        @pl.when(s == 3)
+            bytes_of(fb.at[0:31], f_send.at[0])
+
+        @pl.when(seg != s)
         def _():
-            for i in range(2):
-                bytes_of(xs.at[0, halves[i]], xr_sem.at[3 + i])
-                gather(0, i)
-
-        att = attend(0)
-
-        @pl.when(s == 3)
-        def _():
-            bytes_of(xr, xr_sem.at[1])
-
-        def to_next(i, x, ss):
-            xn[64 * i : 64 * i + 64, :] = x
-            ss = pack_x(1, i, x, column(gain_ref), ss)
-            gather(1, i)
-            return ss
-
-        exchange(0, att, xr, to_next)
-        att = attend(1)
-
-        @pl.when(s == 1)
-        def _():
-            bytes_of(gain3, g_sem.at[3])
-
-            def over(i):
-                rows = halves[i]
-                return rcopy(xs.at[2, rows], xs.at[0, rows], xr_sem.at[2], xr_sem.at[3 + i], (other, 3))
-
-            def to_plane(i, x, ss):
-                xr[64 * i : 64 * i + 64, :] = x
-                ss = pack_x(2, i, x, column(gain3), ss)
-                over(i).start()
-                return ss
-
-            exchange(1, att, xn, to_plane)
-            up = rcopy(xr, xr, xr_sem.at[0], xr_sem.at[1], (other, 3))
-            up.start()
-            bytes_of(xs.at[2], xr_sem.at[2])
-            bytes_of(ub.at[1, 0:15], u_send.at[1])
-            up.wait_send()
-
-        @pl.when(s == 3)
-        def _():
-            att_r = att.T
-            for n in range(4):
-                u = dot(att_r, wob[1, :, n * 512 : (n + 1) * 512], NN)
-                uf[n * NB : (n + 1) * NB] = u.reshape(NB, 4, 512).astype(bf16)
-            sem = f_recv.at[1]
-            dst = fu.at[zl, h]
-            for p in far:
-                for dz in range(2):
-                    for n in range(4):
-                        i = 2 * p + dz
-                        rcopy(uf.at[n * NB + i], dst, f_send.at[1], sem, (i, n)).start()
-            for n in range(4):
-                rcopy(uf.at[n * NB + other], dst, f_send.at[1], sem, (other, n)).start()
-            for n in range(3):
-                rcopy(uf.at[n * NB + b], dst, f_send.at[1], sem, (b, n)).start()
-            pltpu.make_async_copy(uf.at[3 * NB + b], dst, sem).start()
-            bytes_of(uf.at[0:127], f_send.at[1])
-
-            @pl.when(seg == s)
-            def _():
-                bytes_of(fb.at[0:31], f_send.at[0])
-
-            @pl.when(seg != s)
-            def _():
-                bytes_of(fb, f_send.at[0])
-
-        bytes_of(ub.at[0, 0:15], u_send.at[0])
-        for k in range(2):
-            bytes_of(xb.at[k, 0:15], x_send.at[k])
+            bytes_of(fb, f_send.at[0])
+
+        bytes_of(ub.at[:, 0:15], u_send.at[0])
+        bytes_of(xb.at[:, 0:15], x_send.at[0])
 
     bytes_of(qbuf.at[0:31], q_send.at[0])
     bytes_of(ob.at[0:15], r1_sem.at[0])
-    for cp in [kx, vx, gx] + w_away:
+    for cp in [kx, vx] + w_away:
         cp.wait_send()
 
-    @pl.when(c == 0)
-    def _():
-        for cp in w_sib:
+    @pl.when(s != 1)
+    def _():
+        for cp in [gx] + w_same:
             cp.wait_send()
-
-    @pl.when(s == 2)
-    def _():
-        g3.wait_send()
 
     @pl.when(jnp.logical_not(r2_home))
     def _():
@@ -507,33 +462,31 @@
         out_specs=vmem,
         scratch_shapes=[
             pltpu.VMEM((2, LAT), jnp.int32),
-            pltpu.VMEM((1, D), f32),
+            pltpu.VMEM((4, 1, D), f32),
             pltpu.VMEM((NB, 4, D), bf16),
             pltpu.VMEM((2, ROWS, D), bf16),
             pltpu.VMEM((2, ROWS, D), bf16),
             pltpu.VMEM((HEADS, HD, ROWS), bf16),
-            pltpu.VMEM((2, 3, HD, D), bf16),
-            pltpu.VMEM((2, HD, D), bf16),
-            pltpu.VMEM((2, HEADS, HD, HD), bf16),
-            pltpu.VMEM((1, D), f32),
-            pltpu.VMEM((1, D), f32),
+            pltpu.VMEM((4, 3, HD, D), bf16),
+            pltpu.VMEM((4, HD, D), bf16),
+            pltpu.VMEM((3, HEADS, HD, HD), bf16),
             pltpu.VMEM((HEADS, SR, LAT), bf16),
             pltpu.VMEM((HEADS, SR, LAT), bf16),
             pltpu.VMEM((SR, LAT), bf16),
             pltpu.VMEM((4, SR, LAT), bf16),
             pltpu.VMEM((NB, 4, HD), bf16),
-            pltpu.VMEM((3, SR, LAT), bf16),
-            pltpu.VMEM((2, HEADS, SR, LAT), bf16),
-            pltpu.VMEM((HD, LAT), f32),
-            pltpu.VMEM((HD, LAT), f32),
-            pltpu.VMEM((2, HEADS, HD, LAT), bf16),
-            pltpu.VMEM((2, HEADS, HD, LAT), bf16),
+            pltpu.VMEM((4, SR, LAT), bf16),
+            pltpu.VMEM((4, HEADS, SR, LAT), bf16),
+            pltpu.VMEM((4, HD, LAT), f32),
+            pltpu.VMEM((3, HEADS, HD, LAT), bf16),
+            pltpu.VMEM((3, HEADS, HD, LAT), bf16),
             pltpu.VMEM((NB, 4, HD), f32),
             pltpu.VMEM((2, 4, 4, HD), f32),
             pltpu.VMEM((4 * NB, 4, 512), bf16),
             pltpu.VMEM((2, HEADS, 4, 512), bf16),
-            dma((5,)), dma((2,)), dma((2,)), dma((4,)), dma((8,)), dma((4,)), dma((1,)), dma((2,)),
-            dma((2,)), dma((2,)), dma((2,)), dma((2,)), dma((2, 2)), dma((2,)), dma((2, 2)), dma((5,)), dma((2,)), dma((2,)),
+            dma((4,)), dma((2,)), dma((2,)), dma((4,)), dma((8,)), dma((2,)), dma((1,)), dma((2,)),
+            dma((2,)), dma((2,)), dma((2,)), dma((1,)), dma((4, 2)), dma((1,)), dma((3, 2)), dma((2,)), dma((2,)),
+            pltpu.SemaphoreType.REGULAR,
         ],
         compiler_params=pltpu.CompilerParams(
             collective_id=0, has_side_effects=True, vmem_limit_bytes=67043328

time: 84.4 us -> 82.3 us (0.975)
  Pallas kernels: 82.9 us -> 80.8 us
    pallas_call x1, Pallas kernels: 82.9 us -> 80.8 us  [on_device(): pl.pallas_call(kernel, out_shape=jax.ShapeDtypeStruct((2, 4, 512), f32),...]
where the time goes in v5:
time: 82.3 us; the launch traced here: 82.2 us
  Pallas kernels  80.8 us (98%)
  local copies, waits for them, and re-layouts  1.32 us (2%)
    pallas_call x1, Pallas kernels, on_device(): pl.pallas_call(kernel, out_shape=jax.ShapeDtypeStruct((2, 4, 512), f32),...  80.8 us

profile of v5, /device:TPU:1, one launch (start us, length us, event | category | flops | bytes accessed | tf_op | source)
XLA Modules:
  0.0 82.2 jit_solution(9504181782101966900)
XLA Ops:
  0.0 80.8 %ar_step.1 = f32[2,4,512]{2,1,0:T(4,128)} custom-call(bf16[2,4,2048]{2,1,0:T(4,128)(2,1)} %q_hbm.1, bf16[2,4,2048]{2,1,0:T(4,128)(2,1)} %e_hbm.1, bf16[2,256,2048]{2,1,0:T(8,128)(2,1)} %k_hbm.1, bf16[2,256,2048]{2,1,0:T(8,128)(2,1)} %v_hbm.1, s32[2,128]{1,0:T(2,128)} %pos_hbm.1, f32[1,2048]{1,0:T(1,128)} %gain_hbm.1, bf16[3,64,2048]{2,1,0:T(8,128)(2,1)} %bitcast.4, ...), custom_call_target="tpu_custom_call" | custom-call | tf_op jit(solution)/shard_map/ar_step/pallas_call | solution.py:458
  80.8 1.3 %copy.10 = f32[2,4,512]{2,1,0:T(4,128)} copy(f32[2,4,512]{2,1,0:T(4,128)} %ar_step.1) | data formatting | bytes 32768

commit v6 on v5

--- a/solution.py
+++ b/solution.py
@@ -11,7 +11,6 @@
 D = 2048
 ROWS = 256
 NB = 32
-SR = 144
 epsilon = 1e-06
 masked = -1e30
 MESH = pl.DeviceIdType.MESH
@@ -25,7 +24,7 @@
     return sum(min(v, 4 - v) for v in o)
 
 
-FAR = sorted(((dx, dy) for dx in range(4) for dy in range(4) if dx or dy), key=lambda o: -hops(o))
+FAR = [divmod(o, 10) for o in (22, 12, 32, 21, 23, 11, 13, 31, 33, 2, 20, 1, 3, 10, 30)]
 FAR3 = sorted(
     ((dx, dy, dz) for dx in range(4) for dy in range(4) for dz in range(2) if dx or dy or dz),
     key=lambda o: -hops(o),
@@ -33,6 +32,7 @@
 HALVES = [
     sorted(((dx, dy) for dx in steps for dy in range(4)), key=lambda o: -hops(o)) for steps in ((2, 1), (3, 0))
 ]
+NEARS = [divmod(o, 10) for o in (1, 3, 10, 30, 2, 11, 13, 31, 33, 20, 12, 32, 21, 23, 22)]
 NEAR = 10
 
 
@@ -40,27 +40,9 @@
     return lax.dot_general(a, b, dims, preferred_element_type=f32)
 
 
-def split3(v):
-    hi = v.astype(bf16).astype(f32)
-    mid = (v - hi).astype(bf16).astype(f32)
-    return hi, mid, v - hi - mid
-
-
-def stat_rows(*rows):
-    ids = lax.broadcasted_iota(jnp.int32, (16, LAT), 0)
-    out = jnp.zeros((16, LAT), f32)
-    for i, r in enumerate(rows):
-        out = jnp.where(ids == i, jnp.broadcast_to(r, (16, LAT)), out)
-    return out.astype(bf16)
-
-
-def stat3(st, i):
-    return st[i : i + 1] + st[i + 1 : i + 2] + st[i + 2 : i + 3]
-
-
 def kernel(
     q_hbm, e_hbm, k_hbm, v_hbm, pos_hbm, gain_hbm, wt_hbm, wo_hbm, out_ref,
-    pos_ref, gains, qbuf, kb, vb, vts, wt, wob, wot, ob, r1, r2o, r2, ebuf, xs, xb, xf, ub, rb, fb, fx, uf, fu,
+    pos_ref, gains, qbuf, kb, vb, vts, wt, wob, wot, ob, obs, r1, r1s, r2o, r2os, r2, r2s, ebuf, xs, xss, xb, xbs, xf, ub, rb, fb, fx, uf, fu,
     loc_sem, kv_send, kv_recv, w_send, w_recv, g_sem, q_send, q_recv,
     r1_sem, r2_sem, e_sem, x_send, x_recv, u_send, u_recv, f_send, f_recv, go_sem,
 ):
@@ -87,7 +69,7 @@
         return lax.rem(hx + dx, 4) * 4 + lax.rem(hy + dy, 4)
 
     far = [chip(*o) for o in FAR]
-    near = [h] + far[::-1]
+    near = [h] + [chip(*o) for o in NEARS]
 
     half = pl.ds(pl.multiple_of(64 * zl, 64), 64)
     loc = [
@@ -145,11 +127,17 @@
     @pl.when(s != 1)
     def _():
         gx.start()
+
+    @pl.when(c == 0)
+    def _():
         w_away[0].start()
 
+    @pl.when(s != 1)
+    def _():
+        w_away[1].start()
+
     @pl.when(s == 0)
     def _():
-        w_away[1].start()
         for cp in w_same:
             cp.start()
 
@@ -213,60 +201,76 @@
         return top, total, e0.astype(bf16), e1.astype(bf16)
 
     order = [chip(*o) for o in HALVES[0] + HALVES[1]]
-    for g in range(0, HEADS, 2):
+    for g in range(0, HEADS, 4):
         if g == HEADS // 2:
             bytes_of(qbuf.at[0:31, :, 0:1024], q_recv.at[1])
-        group = order[g : g + 2]
+        group = order[g : g + 4]
         ss = [scores(hh) for hh in group]
         ws = [weigh(*v) for v in ss]
         if g == 0:
             vx.wait_recv()
         for hh, (top, total, e0, e1) in zip(group, ws):
             cols = pl.ds(pl.multiple_of(hh * HD, HD), HD)
-            ob[hh, 0:HD, :] = (dot(vts[hh], e0, NN) + dot(vb[1, :, cols].T, e1, NN)).astype(bf16)
-            ob[hh, HD:SR, :] = stat_rows(*split3(top), *split3(total))
-        for i in range(g, g + 2):
+            ob[hh] = (dot(vts[hh], e0, NN) + dot(vb[1, :, cols].T, e1, NN)).astype(bf16)
+            obs[hh, 0:1, :] = top
+            obs[hh, 1:2, :] = total
+        for i in range(g, g + 4):
             if i < HEADS - 1:
                 hh = order[i]
+                rcopy(obs.at[hh], r1s.at[h], r1_sem.at[2], r1_sem.at[3], (hh * 2 + zl, s)).start()
                 rcopy(ob.at[hh], r1.at[h], r1_sem.at[0], r1_sem.at[1], (hh * 2 + zl, s)).start()
 
     bytes_of(r1.at[0:15], r1_sem.at[1])
+    bytes_of(r1s.at[0:15], r1_sem.at[3])
     r1[h] = ob[h]
-
-    def combine(buf, n):
-        st = [buf[i, HD:SR, :].astype(f32) for i in range(n)]
-        tops = [stat3(v, 0) for v in st]
-        top = tops[0]
-        for v in tops[1:]:
-            top = jnp.maximum(top, v)
+    r1s[h] = obs[h]
+
+    def combine(buf, stats, n):
+        top = stats[0, 0:1, :]
+        for i in range(1, n):
+            top = jnp.maximum(top, stats[i, 0:1, :])
         total = jnp.zeros((1, LAT), f32)
         acc = jnp.zeros((HD, LAT), f32)
         for i in range(n):
-            w = jnp.exp(tops[i] - top)
-            total = total + w * stat3(st[i], 3)
-            acc = acc + w * buf[i, 0:HD, :].astype(f32)
+            w = jnp.exp(stats[i, 0:1, :] - top)
+            total = total + w * stats[i, 1:2, :]
+            acc = acc + w * buf[i].astype(f32)
         return acc, top, total
 
-    acc, top, total = combine(r1, HEADS)
-    r2o[0:HD, :] = acc.astype(bf16)
-    r2o[HD:SR, :] = stat_rows(*split3(top), *split3(total))
+    acc, top, total = combine(r1, r1s, HEADS)
+    r2o[...] = acc.astype(bf16)
+    r2os[0:1, :] = top
+    r2os[1:2, :] = total
     z = zh * 2 + zl
     r2_home = (s == 1) & (zl == 1 - c)
     r2_dst = (2 * h + 1 - c, 1)
-    r2_copy = rcopy(r2o, r2.at[z], r2_sem.at[0], r2_sem.at[1], r2_dst)
+    r2_copies = [
+        rcopy(r2os, r2s.at[z], r2_sem.at[2], r2_sem.at[3], r2_dst),
+        rcopy(r2o, r2.at[z], r2_sem.at[0], r2_sem.at[1], r2_dst),
+    ]
 
     @pl.when(r2_home)
     def _():
+        pltpu.make_async_copy(r2os, r2s.at[z], r2_sem.at[3]).start()
         pltpu.make_async_copy(r2o, r2.at[z], r2_sem.at[1]).start()
 
     @pl.when(jnp.logical_not(r2_home))
     def _():
-        r2_copy.start()
-
-    @pl.when(zh == 1)
-    def _():
-        pl.semaphore_wait(go_sem, 2)
-        for cp in [w_away[1]] + w_same:
+        for cp in r2_copies:
+            cp.start()
+
+    @pl.when(s == 2)
+    def _():
+        pl.semaphore_wait(go_sem.at[0], 2)
+        for cp in w_same:
+            cp.start()
+
+    @pl.when(s == 3)
+    def _():
+        pl.semaphore_wait(go_sem.at[0], 2)
+        w_away[0].start()
+        pl.semaphore_wait(go_sem.at[1], 2)
+        for cp in w_same:
             cp.start()
 
     my_cols = pl.ds(pl.multiple_of(h * HD, HD), HD)
@@ -278,19 +282,23 @@
     jj = lax.broadcasted_iota(jnp.int32, (LAT, LAT), 0)
     ii = lax.broadcasted_iota(jnp.int32, (LAT, LAT), 1)
 
-    halves = (slice(0, 64), slice(64, SR))
+    halves = (slice(0, 64), slice(64, HD))
 
     def pack_x(k, i, x, gain, before):
         xs[k, 64 * i : 64 * i + 64, :] = (x * gain[64 * i : 64 * i + 64]).astype(bf16)
         ss = before + jnp.sum(x * x, axis=0, keepdims=True)
         if i:
-            xs[k, HD:SR, :] = stat_rows(*split3(ss))
+            xss[k] = ss
         return ss
 
     def gather(k, i):
         rows = halves[i]
+        if i:
+            for p in far:
+                rcopy(xss.at[k], xbs.at[k, h], x_send.at[1], x_recv.at[k, 2], (p * 2 + zl, s)).start()
+            pltpu.make_async_copy(xss.at[k], xbs.at[k, h], x_recv.at[k, 2]).start()
         for n, p in enumerate(far):
-            late = 1 if n < HEADS - NEAR else 0
+            late = int(FAR[n] in NEARS[NEAR - 1 :])
             rcopy(
                 xs.at[k, rows], xb.at[k, h, rows], x_send.at[0], x_recv.at[k, late], (p * 2 + zl, s)
             ).start()
@@ -316,7 +324,6 @@
                 pltpu.make_async_copy(fb.at[b], dst, sem).start()
 
         qkv = jnp.zeros((3 * HD, LAT), f32)
-        ss = jnp.zeros((1, LAT), f32)
         for j in range(0, HEADS, 2):
             pair = near[j : j + 2]
             if j == 0:
@@ -327,11 +334,10 @@
                     wot[k, i] = wob[k, :, i * HD : (i + 1) * HD].T
                 bytes_of(xb.at[k, 0 : HEADS - NEAR], x_recv.at[k, 1])
             w2 = [wt[k, :, :, pl.ds(pl.multiple_of(p * HD, HD), HD)].reshape(3 * HD, HD) for p in pair]
-            x2 = [xb[k, p, 0:HD, :] for p in pair]
+            x2 = [xb[k, p] for p in pair]
             qkv = qkv + dot(jnp.concatenate(w2, axis=1), jnp.concatenate(x2, axis=0), NN)
-            for p in pair:
-                ss = ss + stat3(xb[k, p, HD:SR, :].astype(f32), 0)
-        factor = lax.rsqrt(ss * (1.0 / D) + epsilon)
+        bytes_of(xbs.at[k], x_recv.at[k, 2])
+        factor = lax.rsqrt(jnp.sum(xbs[k], axis=0) * (1.0 / D) + epsilon)
         qkv = (qkv * factor).astype(bf16)
         qt, kt, vt = qkv[0:HD], qkv[HD : 2 * HD], qkv[2 * HD :]
         sc = dot(kt, qt, TN) * scale
@@ -369,7 +375,8 @@
         bytes_of(ebuf, e_sem.at[1])
         emb = ebuf[...].astype(f32).reshape(LAT, HD).T
         bytes_of(r2, r2_sem.at[1])
-        acc, top, total = combine(r2, 4)
+        bytes_of(r2s, r2_sem.at[3])
+        acc, top, total = combine(r2, r2s, 4)
         x0 = emb + acc / total
         xf[0] = x0
         ss = jnp.zeros((1, LAT), f32)
@@ -377,18 +384,19 @@
             ss = pack_x(0, i, x0[64 * i : 64 * i + 64], column(0), ss)
             gather(0, i)
 
-        def signal(dev):
-            pl.semaphore_signal(go_sem, inc=1, device_id=dev, device_id_type=MESH)
+        def signal(dev, n=0):
+            pl.semaphore_signal(go_sem.at[n], inc=1, device_id=dev, device_id_type=MESH)
 
         signal((other, 1))
-        signal((b, 2))
-        signal((other, 2))
-        pl.semaphore_wait(go_sem, 1)
+        for n in (2, 3):
+            signal((b, n))
+            signal((other, n))
+        pl.semaphore_wait(go_sem.at[0], 1)
         for cp in w_away:
             cp.start()
         exchange(0, attend(0))
-        signal((b, 3))
-        signal((other, 3))
+        signal((b, 3), 1)
+        signal((other, 3), 1)
         for k in range(1, 3):
             exchange(k, attend(k))
         att = attend(3)
@@ -420,9 +428,11 @@
 
         bytes_of(ub.at[:, 0:15], u_send.at[0])
         bytes_of(xb.at[:, 0:15], x_send.at[0])
+        bytes_of(xbs.at[:, 0:15], x_send.at[1])
 
     bytes_of(qbuf.at[0:31], q_send.at[0])
     bytes_of(ob.at[0:15], r1_sem.at[0])
+    bytes_of(obs.at[0:15], r1_sem.at[2])
     for cp in [kx, vx] + w_away:
         cp.wait_send()
 
@@ -433,7 +443,8 @@
 
     @pl.when(jnp.logical_not(r2_home))
     def _():
-        r2_copy.wait_send()
+        for cp in r2_copies:
+            cp.wait_send()
 
     @pl.when(s == 1)
     def _():
@@ -470,13 +481,19 @@
             pltpu.VMEM((4, 3, HD, D), bf16),
             pltpu.VMEM((4, HD, D), bf16),
             pltpu.VMEM((3, HEADS, HD, HD), bf16),
-            pltpu.VMEM((HEADS, SR, LAT), bf16),
-            pltpu.VMEM((HEADS, SR, LAT), bf16),
-            pltpu.VMEM((SR, LAT), bf16),
-            pltpu.VMEM((4, SR, LAT), bf16),
+            pltpu.VMEM((HEADS, HD, LAT), bf16),
+            pltpu.VMEM((HEADS, 2, LAT), f32),
+            pltpu.VMEM((HEADS, HD, LAT), bf16),
+            pltpu.VMEM((HEADS, 2, LAT), f32),
+            pltpu.VMEM((HD, LAT), bf16),
+            pltpu.VMEM((2, LAT), f32),
+            pltpu.VMEM((4, HD, LAT), bf16),
+            pltpu.VMEM((4, 2, LAT), f32),
             pltpu.VMEM((NB, 4, HD), bf16),
-            pltpu.VMEM((4, SR, LAT), bf16),
-            pltpu.VMEM((4, HEADS, SR, LAT), bf16),
+            pltpu.VMEM((4, HD, LAT), bf16),
+            pltpu.VMEM((4, 1, LAT), f32),
+            pltpu.VMEM((4, HEADS, HD, LAT), bf16),
+            pltpu.VMEM((4, HEADS, 1, LAT), f32),
             pltpu.VMEM((4, HD, LAT), f32),
             pltpu.VMEM((3, HEADS, HD, LAT), bf16),
             pltpu.VMEM((3, HEADS, HD, LAT), bf16),
@@ -485,8 +502,8 @@
             pltpu.VMEM((4 * NB, 4, 512), bf16),
             pltpu.VMEM((2, HEADS, 4, 512), bf16),
             dma((4,)), dma((2,)), dma((2,)), dma((4,)), dma((8,)), dma((2,)), dma((1,)), dma((2,)),
-            dma((2,)), dma((2,)), dma((2,)), dma((1,)), dma((4, 2)), dma((1,)), dma((3, 2)), dma((2,)), dma((2,)),
-            pltpu.SemaphoreType.REGULAR,
+            dma((4,)), dma((4,)), dma((2,)), dma((2,)), dma((4, 3)), dma((1,)), dma((3, 2)), dma((2,)), dma((2,)),
+            pltpu.SemaphoreType.REGULAR((2,)),
         ],
         compiler_params=pltpu.CompilerParams(
             collective_id=0, has_side_effects=True, vmem_limit_bytes=67043328

time: 82.3 us -> 79.9 us (0.971)
  Pallas kernels: 80.8 us -> 78.4 us
    pallas_call x1, Pallas kernels: 80.8 us -> 78.4 us  [on_device(): pl.pallas_call(kernel, out_shape=jax.ShapeDtypeStruct((2, 4, 512), f32),...]
where the time goes in v6:
time: 79.9 us; the launch traced here: 79.7 us
  Pallas kernels  78.4 us (98%)
  local copies, waits for them, and re-layouts  1.32 us (2%)
    pallas_call x1, Pallas kernels, on_device(): pl.pallas_call(kernel, out_shape=jax.ShapeDtypeStruct((2, 4, 512), f32),...  78.4 us

profile of v6, /device:TPU:1, one launch (start us, length us, event | category | flops | bytes accessed | tf_op | source)
XLA Modules:
  0.0 79.7 jit_solution(13105253306898728038)
XLA Ops:
  0.0 78.4 %ar_step.1 = f32[2,4,512]{2,1,0:T(4,128)} custom-call(bf16[2,4,2048]{2,1,0:T(4,128)(2,1)} %q_hbm.1, bf16[2,4,2048]{2,1,0:T(4,128)(2,1)} %e_hbm.1, bf16[2,256,2048]{2,1,0:T(8,128)(2,1)} %k_hbm.1, bf16[2,256,2048]{2,1,0:T(8,128)(2,1)} %v_hbm.1, s32[2,128]{1,0:T(2,128)} %pos_hbm.1, f32[1,2048]{1,0:T(1,128)} %gain_hbm.1, bf16[3,64,2048]{2,1,0:T(8,128)(2,1)} %bitcast.4, ...), custom_call_target="tpu_custom_call" | custom-call | tf_op jit(solution)/shard_map/ar_step/pallas_call | solution.py:469
  78.4 1.3 %copy.10 = f32[2,4,512]{2,1,0:T(4,128)} copy(f32[2,4,512]{2,1,0:T(4,128)} %ar_step.1) | data formatting | bytes 32768

commit v7 on v6

--- a/solution.py
+++ b/solution.py
@@ -34,6 +34,8 @@
 ]
 NEARS = [divmod(o, 10) for o in (1, 3, 10, 30, 2, 11, 13, 31, 33, 20, 12, 32, 21, 23, 22)]
 NEAR = 10
+PIECES = 4
+PR = HD // PIECES
 
 
 def dot(a, b, dims):
@@ -282,18 +284,18 @@
     jj = lax.broadcasted_iota(jnp.int32, (LAT, LAT), 0)
     ii = lax.broadcasted_iota(jnp.int32, (LAT, LAT), 1)
 
-    halves = (slice(0, 64), slice(64, HD))
+    pieces = [slice(PR * i, PR * i + PR) for i in range(PIECES)]
 
     def pack_x(k, i, x, gain, before):
-        xs[k, 64 * i : 64 * i + 64, :] = (x * gain[64 * i : 64 * i + 64]).astype(bf16)
+        xs[k, pieces[i], :] = (x * gain[pieces[i]]).astype(bf16)
         ss = before + jnp.sum(x * x, axis=0, keepdims=True)
-        if i:
+        if i == PIECES - 1:
             xss[k] = ss
         return ss
 
     def gather(k, i):
-        rows = halves[i]
-        if i:
+        rows = pieces[i]
+        if i == PIECES - 1:
             for p in far:
                 rcopy(xss.at[k], xbs.at[k, h], x_send.at[1], x_recv.at[k, 2], (p * 2 + zl, s)).start()
             pltpu.make_async_copy(xss.at[k], xbs.at[k, h], x_recv.at[k, 2]).start()
@@ -331,7 +333,9 @@
             if j == NEAR:
                 bytes_of(wob.at[k], w_recv.at[4 + k])
                 for i in range(HEADS if k < 3 else 0):
-                    wot[k, i] = wob[k, :, i * HD : (i + 1) * HD].T
+                    turned = wob[k, :, i * HD : (i + 1) * HD].T
+                    for n, rows in enumerate(pieces):
+                        wot[k, n, i] = turned[rows]
                 bytes_of(xb.at[k, 0 : HEADS - NEAR], x_recv.at[k, 1])
             w2 = [wt[k, :, :, pl.ds(pl.multiple_of(p * HD, HD), HD)].reshape(3 * HD, HD) for p in pair]
             x2 = [xb[k, p] for p in pair]
@@ -347,21 +351,16 @@
         return dot(vt, soft, NN).astype(bf16)
 
     def exchange(k, att):
-        for i in range(2):
-            rows = slice(64 * i, 64 * i + 64)
-            for group in (far[0:5], far[5:15]) if i == 0 else (far,):
-                us = [dot(wot[k, p, rows, :], att, NN).astype(bf16) for p in group]
-                for p, u in zip(group, us):
-                    ub[k, p, rows, :] = u
-                for p in group:
-                    rcopy(
-                        ub.at[k, p, rows], rb.at[k, h, rows], u_send.at[0], u_recv.at[k, i], (p * 2 + zl, s)
-                    ).start()
-        own = dot(wot[k, h], att, NN)
+        for i, rows in enumerate(pieces):
+            u = dot(wot[k, i].reshape(HEADS * PR, HD), att, NN).astype(bf16)
+            ub[k, i] = u.reshape(HEADS, PR, LAT)
+            for p in far:
+                rcopy(
+                    ub.at[k, i, p], rb.at[k, h, rows], u_send.at[0], u_recv.at[k, i], (p * 2 + zl, s)
+                ).start()
         ss = jnp.zeros((1, LAT), f32)
-        for i in range(2):
-            rows = slice(64 * i, 64 * i + 64)
-            x = xf[k, rows, :] + own[rows]
+        for i, rows in enumerate(pieces):
+            x = xf[k, rows, :] + ub[k, i, h].astype(f32)
             bytes_of(rb.at[k, 0:15, rows], u_recv.at[k, i])
             for p in near[1:]:
                 x = x + rb[k, p, rows, :].astype(f32)
@@ -380,8 +379,8 @@
         x0 = emb + acc / total
         xf[0] = x0
         ss = jnp.zeros((1, LAT), f32)
-        for i in range(2):
-            ss = pack_x(0, i, x0[64 * i : 64 * i + 64], column(0), ss)
+        for i, rows in enumerate(pieces):
+            ss = pack_x(0, i, x0[rows], column(0), ss)
             gather(0, i)
 
         def signal(dev, n=0):
@@ -403,14 +402,18 @@
         att_r = att.T
         sem = f_recv.at[1]
         dst = fu.at[1 - zl, h]
+        def hand_out(chips, n):
+            for p in chips:
+                for dz in range(2):
+                    i = 2 * p + dz
+                    rcopy(uf.at[n * NB + i], dst, f_send.at[1], sem, (i, n)).start()
+
         for n in range(4):
             u = dot(att_r, wob[3, :, n * 512 : (n + 1) * 512], NN)
             uf[n * NB : (n + 1) * NB] = u.reshape(NB, 4, 512).astype(bf16)
-        for p in far:
-            for dz in range(2):
-                for n in range(4):
-                    i = 2 * p + dz
-                    rcopy(uf.at[n * NB + i], dst, f_send.at[1], sem, (i, n)).start()
+            hand_out(far[:5], n)
+        for n in range(4):
+            hand_out(far[5:], n)
         for n in range(4):
             rcopy(uf.at[n * NB + other], dst, f_send.at[1], sem, (other, n)).start()
         for n in (0, 2, 3):
@@ -426,7 +429,7 @@
         def _():
             bytes_of(fb, f_send.at[0])
 
-        bytes_of(ub.at[:, 0:15], u_send.at[0])
+        bytes_of(ub.at[:, :, 0:15], u_send.at[0])
         bytes_of(xb.at[:, 0:15], x_send.at[0])
         bytes_of(xbs.at[:, 0:15], x_send.at[1])
 
@@ -480,7 +483,7 @@
             pltpu.VMEM((HEADS, HD, ROWS), bf16),
             pltpu.VMEM((4, 3, HD, D), bf16),
             pltpu.VMEM((4, HD, D), bf16),
-            pltpu.VMEM((3, HEADS, HD, HD), bf16),
+            pltpu.VMEM((3, PIECES, HEADS, PR, HD), bf16),
             pltpu.VMEM((HEADS, HD, LAT), bf16),
             pltpu.VMEM((HEADS, 2, LAT), f32),
             pltpu.VMEM((HEADS, HD, LAT), bf16),
@@ -495,14 +498,14 @@
             pltpu.VMEM((4, HEADS, HD, LAT), bf16),
             pltpu.VMEM((4, HEADS, 1, LAT), f32),
             pltpu.VMEM((4, HD, LAT), f32),
-            pltpu.VMEM((3, HEADS, HD, LAT), bf16),
+            pltpu.VMEM((3, PIECES, HEADS, PR, LAT), bf16),
             pltpu.VMEM((3, HEADS, HD, LAT), bf16),
             pltpu.VMEM((NB, 4, HD), f32),
             pltpu.VMEM((2, 4, 4, HD), f32),
             pltpu.VMEM((4 * NB, 4, 512), bf16),
             pltpu.VMEM((2, HEADS, 4, 512), bf16),
             dma((4,)), dma((2,)), dma((2,)), dma((4,)), dma((8,)), dma((2,)), dma((1,)), dma((2,)),
-            dma((4,)), dma((4,)), dma((2,)), dma((2,)), dma((4, 3)), dma((1,)), dma((3, 2)), dma((2,)), dma((2,)),
+            dma((4,)), dma((4,)), dma((2,)), dma((2,)), dma((4, 3)), dma((1,)), dma((3, PIECES)), dma((2,)), dma((2,)),
             pltpu.SemaphoreType.REGULAR((2,)),
         ],
         compiler_params=pltpu.CompilerParams(

time: 79.9 us -> 79.2 us (level)
  Pallas kernels: 78.4 us -> 77.6 us
where the time goes in v7:
time: 79.2 us; the launch traced here: 79 us
  Pallas kernels  77.6 us (98%)
  local copies, waits for them, and re-layouts  1.32 us (2%)
    pallas_call x1, Pallas kernels, on_device(): pl.pallas_call(kernel, out_shape=jax.ShapeDtypeStruct((2, 4, 512), f32),...  77.6 us

profile of v7, /device:TPU:1, one launch (start us, length us, event | category | flops | bytes accessed | tf_op | source)
XLA Modules:
  0.0 79.0 jit_solution(7015030777095084027)
XLA Ops:
  0.0 77.6 %ar_step.1 = f32[2,4,512]{2,1,0:T(4,128)} custom-call(bf16[2,4,2048]{2,1,0:T(4,128)(2,1)} %q_hbm.1, bf16[2,4,2048]{2,1,0:T(4,128)(2,1)} %e_hbm.1, bf16[2,256,2048]{2,1,0:T(8,128)(2,1)} %k_hbm.1, bf16[2,256,2048]{2,1,0:T(8,128)(2,1)} %v_hbm.1, s32[2,128]{1,0:T(2,128)} %pos_hbm.1, f32[1,2048]{1,0:T(1,128)} %gain_hbm.1, bf16[3,64,2048]{2,1,0:T(8,128)(2,1)} %bitcast.4, ...), custom_call_target="tpu_custom_call" | custom-call | tf_op jit(solution)/shard_map/ar_step/pallas_call | solution.py:472
  77.7 1.3 %copy.10 = f32[2,4,512]{2,1,0:T(4,128)} copy(f32[2,4,512]{2,1,0:T(4,128)} %ar_step.1) | data formatting | bytes 32768

commit v8 on v7

--- a/solution.py
+++ b/solution.py
@@ -34,7 +34,7 @@
 ]
 NEARS = [divmod(o, 10) for o in (1, 3, 10, 30, 2, 11, 13, 31, 33, 20, 12, 32, 21, 23, 22)]
 NEAR = 10
-PIECES = 4
+PIECES = 8
 PR = HD // PIECES
 
 
@@ -297,14 +297,14 @@
         rows = pieces[i]
         if i == PIECES - 1:
             for p in far:
-                rcopy(xss.at[k], xbs.at[k, h], x_send.at[1], x_recv.at[k, 2], (p * 2 + zl, s)).start()
-            pltpu.make_async_copy(xss.at[k], xbs.at[k, h], x_recv.at[k, 2]).start()
+                rcopy(xss.at[k], xbs.at[k, h], x_send.at[1], x_recv.at[2], (p * 2 + zl, s)).start()
+            pltpu.make_async_copy(xss.at[k], xbs.at[k, h], x_recv.at[2]).start()
         for n, p in enumerate(far):
             late = int(FAR[n] in NEARS[NEAR - 1 :])
             rcopy(
-                xs.at[k, rows], xb.at[k, h, rows], x_send.at[0], x_recv.at[k, late], (p * 2 + zl, s)
+                xs.at[k, rows], xb.at[k, h, rows], x_send.at[0], x_recv.at[late], (p * 2 + zl, s)
             ).start()
-        pltpu.make_async_copy(xs.at[k, rows], xb.at[k, h, rows], x_recv.at[k, 0]).start()
+        pltpu.make_async_copy(xs.at[k, rows], xb.at[k, h, rows], x_recv.at[0]).start()
 
     def attend(k):
         bytes_of(wt.at[k], w_recv.at[k])
@@ -329,18 +329,18 @@
         for j in range(0, HEADS, 2):
             pair = near[j : j + 2]
             if j == 0:
-                bytes_of(xb.at[k, 0:NEAR], x_recv.at[k, 0])
+                bytes_of(xb.at[k, 0:NEAR], x_recv.at[0])
             if j == NEAR:
                 bytes_of(wob.at[k], w_recv.at[4 + k])
                 for i in range(HEADS if k < 3 else 0):
                     turned = wob[k, :, i * HD : (i + 1) * HD].T
                     for n, rows in enumerate(pieces):
                         wot[k, n, i] = turned[rows]
-                bytes_of(xb.at[k, 0 : HEADS - NEAR], x_recv.at[k, 1])
+                bytes_of(xb.at[k, 0 : HEADS - NEAR], x_recv.at[1])
             w2 = [wt[k, :, :, pl.ds(pl.multiple_of(p * HD, HD), HD)].reshape(3 * HD, HD) for p in pair]
             x2 = [xb[k, p] for p in pair]
             qkv = qkv + dot(jnp.concatenate(w2, axis=1), jnp.concatenate(x2, axis=0), NN)
-        bytes_of(xbs.at[k], x_recv.at[k, 2])
+        bytes_of(xbs.at[k], x_recv.at[2])
         factor = lax.rsqrt(jnp.sum(xbs[k], axis=0) * (1.0 / D) + epsilon)
         qkv = (qkv * factor).astype(bf16)
         qt, kt, vt = qkv[0:HD], qkv[HD : 2 * HD], qkv[2 * HD :]
@@ -356,12 +356,12 @@
             ub[k, i] = u.reshape(HEADS, PR, LAT)
             for p in far:
                 rcopy(
-                    ub.at[k, i, p], rb.at[k, h, rows], u_send.at[0], u_recv.at[k, i], (p * 2 + zl, s)
+                    ub.at[k, i, p], rb.at[k, h, rows], u_send.at[0], u_recv.at[i], (p * 2 + zl, s)
                 ).start()
         ss = jnp.zeros((1, LAT), f32)
         for i, rows in enumerate(pieces):
             x = xf[k, rows, :] + ub[k, i, h].astype(f32)
-            bytes_of(rb.at[k, 0:15, rows], u_recv.at[k, i])
+            bytes_of(rb.at[k, 0:15, rows], u_recv.at[i])
             for p in near[1:]:
                 x = x + rb[k, p, rows, :].astype(f32)
             xf[k + 1, rows, :] = x
@@ -505,7 +505,7 @@
             pltpu.VMEM((4 * NB, 4, 512), bf16),
             pltpu.VMEM((2, HEADS, 4, 512), bf16),
             dma((4,)), dma((2,)), dma((2,)), dma((4,)), dma((8,)), dma((2,)), dma((1,)), dma((2,)),
-            dma((4,)), dma((4,)), dma((2,)), dma((2,)), dma((4, 3)), dma((1,)), dma((3, PIECES)), dma((2,)), dma((2,)),
+            dma((4,)), dma((4,)), dma((2,)), dma((2,)), dma((3,)), dma((1,)), dma((PIECES,)), dma((2,)), dma((2,)),
             pltpu.SemaphoreType.REGULAR((2,)),
         ],
         compiler_params=pltpu.CompilerParams(

time: 79.2 us -> 78.7 us (level)
  no operation moved by 1% of the time
where the time goes in v8:
time: 78.7 us; the launch traced here: 78.5 us
  Pallas kernels  77.2 us (98%)
  local copies, waits for them, and re-layouts  1.32 us (2%)
    pallas_call x1, Pallas kernels, on_device(): pl.pallas_call(kernel, out_shape=jax.ShapeDtypeStruct((2, 4, 512), f32),...  77.2 us

profile of v8, /device:TPU:1, one launch (start us, length us, event | category | flops | bytes accessed | tf_op | source)
XLA Modules:
  0.0 78.5 jit_solution(17973096905628172214)
XLA Ops:
  0.0 77.2 %ar_step.1 = f32[2,4,512]{2,1,0:T(4,128)} custom-call(bf16[2,4,2048]{2,1,0:T(4,128)(2,1)} %q_hbm.1, bf16[2,4,2048]{2,1,0:T(4,128)(2,1)} %e_hbm.1, bf16[2,256,2048]{2,1,0:T(8,128)(2,1)} %k_hbm.1, bf16[2,256,2048]{2,1,0:T(8,128)(2,1)} %v_hbm.1, s32[2,128]{1,0:T(2,128)} %pos_hbm.1, f32[1,2048]{1,0:T(1,128)} %gain_hbm.1, bf16[3,64,2048]{2,1,0:T(8,128)(2,1)} %bitcast.4, ...), custom_call_target="tpu_custom_call" | custom-call | tf_op jit(solution)/shard_map/ar_step/pallas_call | solution.py:472
  77.2 1.3 %copy.10 = f32[2,4,512]{2,1,0:T(4,128)} copy(f32[2,4,512]{2,1,0:T(4,128)} %ar_step.1) | data formatting | bytes 32768

commit v9 on v8

--- a/solution.py
+++ b/solution.py
@@ -293,8 +293,7 @@
             xss[k] = ss
         return ss
 
-    def gather(k, i):
-        rows = pieces[i]
+    def gather(k, i, rows):
         if i == PIECES - 1:
             for p in far:
                 rcopy(xss.at[k], xbs.at[k, h], x_send.at[1], x_recv.at[2], (p * 2 + zl, s)).start()
@@ -366,7 +365,7 @@
                 x = x + rb[k, p, rows, :].astype(f32)
             xf[k + 1, rows, :] = x
             ss = pack_x(k + 1, i, x, column(k + 1), ss)
-            gather(k + 1, i)
+            gather(k + 1, i, rows)
 
     @pl.when(s == 1)
     def _():
@@ -381,7 +380,7 @@
         ss = jnp.zeros((1, LAT), f32)
         for i, rows in enumerate(pieces):
             ss = pack_x(0, i, x0[rows], column(0), ss)
-            gather(0, i)
+        gather(0, PIECES - 1, slice(0, HD))
 
         def signal(dev, n=0):
             pl.semaphore_signal(go_sem.at[n], inc=1, device_id=dev, device_id_type=MESH)

time: 78.7 us -> 78.3 us (level)
  no operation moved by 1% of the time
where the time goes in v9:
time: 78.3 us; the launch traced here: 78.1 us
  Pallas kernels  76.8 us (98%)
  local copies, waits for them, and re-layouts  1.32 us (2%)
    pallas_call x1, Pallas kernels, on_device(): pl.pallas_call(kernel, out_shape=jax.ShapeDtypeStruct((2, 4, 512), f32),...  76.8 us

profile of v9, /device:TPU:1, one launch (start us, length us, event | category | flops | bytes accessed | tf_op | source)
XLA Modules:
  0.0 78.1 jit_solution(11038835345107844180)
XLA Ops:
  0.0 76.8 %ar_step.1 = f32[2,4,512]{2,1,0:T(4,128)} custom-call(bf16[2,4,2048]{2,1,0:T(4,128)(2,1)} %q_hbm.1, bf16[2,4,2048]{2,1,0:T(4,128)(2,1)} %e_hbm.1, bf16[2,256,2048]{2,1,0:T(8,128)(2,1)} %k_hbm.1, bf16[2,256,2048]{2,1,0:T(8,128)(2,1)} %v_hbm.1, s32[2,128]{1,0:T(2,128)} %pos_hbm.1, f32[1,2048]{1,0:T(1,128)} %gain_hbm.1, bf16[3,64,2048]{2,1,0:T(8,128)(2,1)} %bitcast.4, ...), custom_call_target="tpu_custom_call" | custom-call | tf_op jit(solution)/shard_map/ar_step/pallas_call | solution.py:471
  76.8 1.3 %copy.10 = f32[2,4,512]{2,1,0:T(4,128)} copy(f32[2,4,512]{2,1,0:T(4,128)} %ar_step.1) | data formatting | bytes 32768
